TPU v7x, 32 devices: a whole 2x2x4 slice. The times are simulated.
32 devices in a mesh: grp: 2 (over y), seq: 4 (over z), head: 2 (over x), clip: 2 (over core).
Axes of the slice: x: 2, y: 2, z: 4, core: 2. Of those that a mesh axis runs over, the one named last changes fastest.
Arguments:
- query_states: bfloat16 [4, 2048, 1536], P(('grp', 'clip'), 'seq', 'head'), parts along dimension 0, may hold values from -64 to 64
- key_states: bfloat16 [4, 2048, 1536], P(('grp', 'clip'), 'seq', 'head'), parts along dimension 0, may hold values from -4 to 4
- value_states: bfloat16 [4, 2048, 1536], P(('grp', 'clip'), 'seq', 'head'), parts along dimension 0, may hold values from -5 to 5
- output_grad: bfloat16 [4, 2048, 3072], P(('grp', 'clip'), 'seq', 'head'), parts along dimension 0, may hold values from -48 to 48
- w_out: bfloat16 [1536, 3072], P('head'), may hold values from -0.15625 to 0.15625
- key_list: int32 [4, 8, 8], P(('grp', 'clip')), parts along dimension 0, may hold values from 0 to 7, as said below
- key_count: int32 [4, 8], P(('grp', 'clip')), parts along dimension 0, may hold values from 1 to 8, as said below
Outputs:
- query_grad: bfloat16 [4, 2048, 1536], P(('grp', 'clip'), 'seq', 'head'), parts along dimension 0
- key_grad: bfloat16 [4, 2048, 1536], P(('grp', 'clip'), 'seq', 'head'), parts along dimension 0
- value_grad: bfloat16 [4, 2048, 1536], P(('grp', 'clip'), 'seq', 'head'), parts along dimension 0
- grad_features: float32 [4, 12, 3], P(('grp', 'clip'), 'head'), parts along dimension 0
There are 2 independent parts, one for each index of `grp`. A program takes and returns all parts, laid end to end along the dimension named above; an argument that names none is the same for every part. Nothing has to cross between parts.
Inputs may be any that keep to these rules, and one draw needn't show every extreme that they name: Tile i lies in frame block i // 4 at place i % 4. For each clip and query tile i the first key_count entries of key_list are distinct key tiles in ascending order, among them i itself, each at a place within 2 of i's place, in i's frame block or in the other one; the remaining entries equal i. `key_count`: in every draw some query tile lists 8 key tiles.
All inputs are finite; a program needn't handle non-finite values.
Results may differ from a plain program's by a relative error of at most 0.035.
Values may be sent and summed in bfloat16 or wider, within the bound.
No kernel may reach another device: no remote copies, remote signals or barrier semaphores. Data moves between devices by JAX's collectives and lax.ppermute only.
A program may use at most 128 MiB of HBM per device.

v0:
```python
import jax
import jax.numpy as jnp
from jax import lax
from jax.sharding import PartitionSpec as P

HD = 128
TILE = 256


def attend(query_tiles, key_buf, value_buf, grad_tiles, buf_slots, counts):
    score_scale = HD ** (-0.5)
    tile_count, tile_rows, feat_width = query_tiles.shape
    slot_count = buf_slots.shape[1]
    key_span = slot_count * tile_rows
    buf_tiles = key_buf.shape[0]
    key_sel = key_buf[buf_slots].reshape(tile_count, key_span, feat_width)
    value_sel = value_buf[buf_slots].reshape(tile_count, key_span, feat_width)
    allowed = jnp.arange(key_span)[None, :] // tile_rows < counts[:, None]

    def head_step(head_idx, carried):
        query_acc, key_acc, value_acc = carried
        col_start = head_idx * HD
        query_head = lax.dynamic_slice_in_dim(query_tiles, col_start, HD, 2)
        key_head = lax.dynamic_slice_in_dim(key_sel, col_start, HD, 2)
        value_head = lax.dynamic_slice_in_dim(value_sel, col_start, HD, 2)
        grad_head = lax.dynamic_slice_in_dim(grad_tiles, col_start, HD, 2)
        scores = (
            jnp.einsum("iqe,ike->iqk", query_head, key_head, preferred_element_type=jnp.float32)
            * score_scale
        )
        scores = jnp.where(allowed[:, None, :], scores, -jnp.inf)
        row_max = jnp.max(scores, axis=-1, keepdims=True)
        log_norm = row_max + jnp.log(jnp.sum(jnp.exp(scores - row_max), axis=-1, keepdims=True))
        weights = jnp.exp(scores - log_norm)
        weights_b = weights.astype(jnp.bfloat16)
        attn_out = jnp.einsum(
            "iqk,ike->iqe", weights_b, value_head, preferred_element_type=jnp.float32
        ).astype(jnp.bfloat16)
        row_delta = jnp.sum(
            grad_head.astype(jnp.float32) * attn_out.astype(jnp.float32), axis=-1, keepdims=True
        )
        dprob = jnp.einsum(
            "iqe,ike->iqk", grad_head, value_head, preferred_element_type=jnp.float32
        )
        dscore = (weights * (dprob - row_delta)).astype(jnp.bfloat16)
        query_head_grad = score_scale * jnp.einsum(
            "iqk,ike->iqe", dscore, key_head, preferred_element_type=jnp.float32
        )
        key_head_grad = score_scale * jnp.einsum(
            "iqk,iqe->ike", dscore, query_head, preferred_element_type=jnp.float32
        )
        value_head_grad = jnp.einsum(
            "iqk,iqe->ike", weights_b, grad_head, preferred_element_type=jnp.float32
        )
        query_acc = lax.dynamic_update_slice_in_dim(query_acc, query_head_grad, col_start, 2)
        key_acc = lax.dynamic_update_slice_in_dim(key_acc, key_head_grad, col_start, 2)
        value_acc = lax.dynamic_update_slice_in_dim(value_acc, value_head_grad, col_start, 2)
        return (query_acc, key_acc, value_acc)

    start_state = (
        jnp.zeros((tile_count, tile_rows, feat_width), jnp.float32),
        jnp.zeros((tile_count, key_span, feat_width), jnp.float32),
        jnp.zeros((tile_count, key_span, feat_width), jnp.float32),
    )
    query_full, key_sel_grad, value_sel_grad = lax.fori_loop(
        0, feat_width // HD, head_step, start_state
    )
    live_slot = jnp.arange(slot_count)[None, :] < counts[:, None]
    routing = (
        (buf_slots[:, :, None] == jnp.arange(buf_tiles)[None, None, :]) & live_slot[:, :, None]
    ).astype(jnp.float32)
    key_grad_buf = jnp.einsum(
        "imb,imr->br",
        routing,
        key_sel_grad.reshape(tile_count, slot_count, tile_rows * feat_width),
        precision=lax.Precision.HIGHEST,
    )
    value_grad_buf = jnp.einsum(
        "imb,imr->br",
        routing,
        value_sel_grad.reshape(tile_count, slot_count, tile_rows * feat_width),
        precision=lax.Precision.HIGHEST,
    )
    return (
        query_full,
        key_grad_buf.reshape(buf_tiles, tile_rows, feat_width),
        value_grad_buf.reshape(buf_tiles, tile_rows, feat_width),
    )


def head_squares(grads_full, head_count):
    rows = grads_full.reshape(-1, head_count, HD)
    return jnp.sum(rows * rows, axis=(0, 2))


def per_device(query_states, key_states, value_states, output_grad, w_out, key_list, key_count):
    seq_count = lax.axis_size("seq")
    seq_index = lax.axis_index("seq")
    tok_rows = query_states.shape[1]
    feat_width = query_states.shape[2]
    head_count = feat_width // HD
    tile_count = tok_rows // TILE
    first_tile = seq_index * tile_count
    own_lists = lax.dynamic_slice_in_dim(key_list[0], first_tile, tile_count, 0)
    own_counts = lax.dynamic_slice_in_dim(key_count[0], first_tile, tile_count, 0)
    grad_out = lax.dot_general(
        lax.all_gather(output_grad, "head", axis=2, tiled=True)[0],
        w_out,
        (((1,), (1,)), ((), ())),
        preferred_element_type=jnp.float32,
    ).astype(jnp.bfloat16)
    query_tiles = query_states[0].reshape(tile_count, TILE, feat_width)
    grad_tiles = grad_out.reshape(tile_count, TILE, feat_width)
    key_whole, value_whole = (
        lax.all_gather(key_states, "seq", axis=1, tiled=True),
        lax.all_gather(value_states, "seq", axis=1, tiled=True),
    )
    key_buf = key_whole[0].reshape(-1, TILE, feat_width)
    value_buf = value_whole[0].reshape(-1, TILE, feat_width)
    query_full, key_grad_buf, value_grad_buf = attend(
        query_tiles, key_buf, value_buf, grad_tiles, own_lists, own_counts
    )
    buf_rows = key_grad_buf.shape[0] * TILE
    key_sum, value_sum = (
        lax.psum_scatter(
            key_grad_buf.reshape(1, buf_rows, feat_width).astype(jnp.bfloat16),
            "seq",
            scatter_dimension=1,
            tiled=True,
        ).astype(jnp.float32),
        lax.psum_scatter(
            value_grad_buf.reshape(1, buf_rows, feat_width).astype(jnp.bfloat16),
            "seq",
            scatter_dimension=1,
            tiled=True,
        ).astype(jnp.float32),
    )
    key_full = key_sum[0]
    value_full = value_sum[0]
    query_rows = query_full.reshape(tok_rows, feat_width)
    local_sums = jnp.stack(
        [
            head_squares(query_rows, head_count),
            head_squares(key_full, head_count),
            head_squares(value_full, head_count),
        ],
        axis=-1,
    )
    total_sums = lax.psum(local_sums, "seq")
    grad_features = jnp.log(total_sums / (seq_count * tok_rows * HD) + 1e-06)
    return (
        query_rows.astype(jnp.bfloat16)[None],
        key_full.astype(jnp.bfloat16)[None],
        value_full.astype(jnp.bfloat16)[None],
        grad_features[None],
    )


def solution(mesh):
    in_specs = (
        P(("grp", "clip"), "seq", "head"),
        P(("grp", "clip"), "seq", "head"),
        P(("grp", "clip"), "seq", "head"),
        P(("grp", "clip"), "seq", "head"),
        P("head", None),
        P(("grp", "clip"), None, None),
        P(("grp", "clip"), None),
    )
    out_specs = (
        P(("grp", "clip"), "seq", "head"),
        P(("grp", "clip"), "seq", "head"),
        P(("grp", "clip"), "seq", "head"),
        P(("grp", "clip"), "head", None),
    )
    return jax.shard_map(
        per_device, mesh=mesh, in_specs=in_specs, out_specs=out_specs, check_vma=False
    )
```

profile of v0, /device:TPU:4, one launch (start us, length us, event | category | flops | bytes accessed | tf_op | source)
XLA Modules:
  0.0 459.9 jit_solution(8411246772068753391)
XLA Ops:
  11.1 44.6 %all-gather.6.cloned.1.call-done = bf16[1,512,3072]{2,1,0:T(8,128)(2,1)} async-done(((bf16[1,512,1536]{2,1,0:T(8,128)(2,1)}), bf16[1,512,3072]{2,1,0:T(8,128)(2,1)}) %all-gather.6.cloned.1.call-update) | async-done | bytes 3145744 | tf_op jit(solution)/shard_map/all_gather | solution.py:107
  55.7 5.9 %fusion.28 = bf16[512,768]{1,0:T(8,128)(2,1)S(1)} fusion(bf16[768,3072]{1,0:T(8,128)(2,1)} %param.13, bf16[1,512,3072]{2,1,0:T(8,128)(2,1)} %all-gather.6.cloned.1.call-done), kind=kOutput, calls=%fused_computation.42 | convolution fusion | flops 2416312320 | bytes 8650752 | tf_op jit(solution)/shard_map/dot_general | solution.py:106
  61.7 59.1 %all-gather.4.cloned.1.call-done = bf16[1,2048,768]{2,1,0:T(8,128)(2,1)} async-done(((bf16[1,512,768]{2,1,0:T(8,128)(2,1)}), bf16[1,2048,768]{2,1,0:T(8,128)(2,1)}) %all-gather.4.cloned.1.call-update) | async-done | bytes 3145744 | tf_op jit(solution)/shard_map/all_gather | solution.py:115
  120.8 5.6 %gather_fusion = bf16[16,256,768]{2,1,0:T(8,128)(2,1)} fusion(bf16[8,256,768]{2,1,0:T(8,128)(2,1)} %bitcast.50, s32[1024]{0:T(1024)S(1)} %pad_clamp_fusion), kind=kCustom, calls=%fused_computation | custom fusion | bytes 12582976 | tf_op jit(solution)/shard_map/gather | solution.py:16
  126.3 58.1 %all-gather.8.cloned.1.call-done = bf16[1,2048,768]{2,1,0:T(8,128)(2,1)} async-done(((bf16[1,512,768]{2,1,0:T(8,128)(2,1)}), bf16[1,2048,768]{2,1,0:T(8,128)(2,1)}) %all-gather.8.cloned.1.call-update) | async-done | bytes 3145744 | tf_op jit(solution)/shard_map/all_gather | solution.py:116
  184.5 5.5 %gather_fusion.1 = bf16[16,256,768]{2,1,0:T(8,128)(2,1)} fusion(bf16[8,256,768]{2,1,0:T(8,128)(2,1)} %bitcast.51, s32[1024]{0:T(1024)S(1)} %pad_clamp_fusion), kind=kCustom, calls=%fused_computation.1 | custom fusion | bytes 12582976 | tf_op jit(solution)/shard_map/gather | solution.py:17
  190.0 5.4 %broadcast.103 = f32[2,2048,768]{2,1,0:T(8,128)} broadcast(f32[]{:T(128)} %constant.78.clone.1), dimensions={} | broadcast | bytes 12582916 | tf_op jit(solution)/shard_map/broadcast.13
  195.4 5.3 %broadcast.103.clone = f32[2,2048,768]{2,1,0:T(8,128)} broadcast(f32[]{:T(128)} %constant.78.clone.1), dimensions={} | broadcast | bytes 12582916 | tf_op jit(solution)/shard_map/broadcast.13
  200.8 92.5 %while.18 = (s32[]{:T(128)}, f32[2,256,768]{2,1,0:T(8,128)S(1)}, f32[2,2048,768]{2,1,0:T(8,128)}, f32[2,2048,768]{2,1,0:T(8,128)}, bf16[2,256,768]{2,1,0:T(8,128...) while((s32[]{:T(128)}, f32[2,256,768]{2,1,0:T(8,128)S(1)}, ...), condition=%wide.region_4.5_spmd.clone, body=%wide.region_0.4_spmd.clone.sunk | while | flops 1625164800 | bytes 36614328 | solution.py:65
  201.1 2.1 fusion.71
  203.2 0.7 exponential_reduce_fusion.2
  203.9 2.6 convolution_dynamic-update-slice_fusion.2
  206.5 2.2 fusion.72
  208.7 2.3 multiply_convert_fusion.2
  211.0 3.4 fusion.74
  214.4 1.9 fusion.73
  216.4 2.1 fusion.71
  218.5 0.7 exponential_reduce_fusion.2
  219.2 2.6 convolution_dynamic-update-slice_fusion.2
  221.9 2.2 fusion.72
  224.1 2.3 multiply_convert_fusion.2
  226.4 3.3 fusion.74
  229.7 1.9 fusion.73
  231.7 2.1 fusion.71
  233.8 0.7 exponential_reduce_fusion.2
  234.6 2.7 convolution_dynamic-update-slice_fusion.2
  237.2 2.2 fusion.72
  239.4 2.3 multiply_convert_fusion.2
  241.7 3.3 fusion.74
  245.0 1.9 fusion.73
  247.1 2.1 fusion.71
  249.9 2.8 convolution_dynamic-update-slice_fusion.2
  252.7 2.2 fusion.72
  254.9 2.3 multiply_convert_fusion.2
  257.1 3.4 fusion.74
  260.6 1.9 fusion.73
  262.6 2.1 fusion.71
  264.7 0.7 exponential_reduce_fusion.2
  265.4 2.7 convolution_dynamic-update-slice_fusion.2
  268.1 2.2 fusion.72
  270.3 2.3 multiply_convert_fusion.2
  272.6 3.4 fusion.74
  276.0 1.9 fusion.73
  278.0 2.1 fusion.71
  280.1 0.7 exponential_reduce_fusion.2
  280.9 2.6 convolution_dynamic-update-slice_fusion.2
  283.5 2.2 fusion.72
  285.7 2.3 multiply_convert_fusion.2
  288.0 3.4 fusion.74
  291.3 1.9 fusion.73
  293.3 1.1 copy-done.2
  294.4 13.2 %reshape.176 = f32[2,8,196608]{2,1,0:T(8,128)} reshape(f32[2,2048,768]{2,1,0:T(8,128)} %get-tuple-element.161) | data formatting | bytes 25165824 | tf_op jit(solution)/shard_map/reshape | solution.py:75
  307.6 7.6 %fusion.24 = bf16[8,196608]{1,0:T(8,128)(2,1)S(1)} fusion(f32[2,8,196608]{2,1,0:T(8,128)} %reshape.176, s32[2,8]{1,0:T(2,128)S(1)} %dynamic-slice_bitcast_fusion, pred[2,8]{1,0:T(4,128)(4,1)S(1)} %iota_compare_fusion.1), kind=kOutput, calls=%fused_computation.35 | convolution fusion | flops 303563008 | bytes 15728720 | tf_op jit(solution)/shard_map/imb,imr->br/dot_general | solution.py:72
  315.2 3.2 convert_element_type.94
  318.5 13.3 %reshape.177 = f32[2,8,196608]{2,1,0:T(8,128)} reshape(f32[2,2048,768]{2,1,0:T(8,128)} %get-tuple-element.162) | data formatting | bytes 25165824 | tf_op jit(solution)/shard_map/reshape | solution.py:81
  331.8 7.6 %fusion.25 = bf16[8,196608]{1,0:T(8,128)(2,1)S(1)} fusion(f32[2,8,196608]{2,1,0:T(8,128)} %reshape.177, s32[2,8]{1,0:T(2,128)S(1)} %dynamic-slice_bitcast_fusion, pred[2,8]{1,0:T(4,128)(4,1)S(1)} %iota_compare_fusion.1), kind=kOutput, calls=%fused_computation.36 | convolution fusion | flops 303563008 | bytes 15728720 | tf_op jit(solution)/shard_map/imb,imr->br/dot_general | solution.py:78
  339.4 3.1 convert_element_type.96
  342.5 1.4 copy-done.3
  343.9 1.0 multiply_reduce_fusion.2
  345.1 32.6 %reduce-scatter.3.cloned.1.call-done = bf16[1,512,768]{2,1,0:T(8,128)(2,1)} async-done(((bf16[1,2048,768]{2,1,0:T(8,128)(2,1)}), bf16[1,512,768]{2,1,0:T(8,128)(2,1)}) %reduce-scatter.3.cloned.1.call-update) | async-done | bytes 786448 | tf_op jit(solution)/shard_map/reduce_scatter | solution.py:125
  377.6 1.3 multiply_reduce_fusion.1
  379.1 61.6 %reduce-scatter.5.cloned.1.call-done = bf16[1,512,768]{2,1,0:T(8,128)(2,1)} async-done(((bf16[1,2048,768]{2,1,0:T(8,128)(2,1)}), bf16[1,512,768]{2,1,0:T(8,128)(2,1)}) %reduce-scatter.5.cloned.1.call-update) | async-done | bytes 786448 | tf_op jit(solution)/shard_map/reduce_scatter | solution.py:131
  440.7 1.3 multiply_reduce_fusion
  442.2 10.6 %psum.7 = f32[6,3]{0,1:T(4,128)S(1)} all-reduce(f32[6,3]{0,1:T(4,128)S(1)} %pad_maximum_fusion), channel_id=1, replica_groups=mesh['grp'=2,'seq'=4,'head'=2,'clip'=2] {'seq'}, use_global_device_ids=true, to_apply=%region_13.14 | all-reduce | flops 18 | bytes 144 | tf_op jit(solution)/shard_map/psum | solution.py:149
  (43 shorter events, 6.2 us)
Async XLA Ops:
  7.2 3.1 copy-start
  7.2 48.6 %all-gather.6.cloned.1.call-start = ((), (), s32[]{:S(2)}) async-start(), calls=%async_computation.3 | async-start | bytes 4718592 | tf_op jit(solution)/shard_map/all_gather | solution.py:107
  7.9 112.9 %all-gather.4.cloned.1.call-start = ((), (), s32[]{:S(2)}) async-start(), calls=%async_computation.2 | async-start | bytes 3932160 | tf_op jit(solution)/shard_map/all_gather | solution.py:115
  8.7 175.8 %all-gather.8.cloned.1.call-start = ((), (), s32[]{:S(2)}) async-start(), calls=%async_computation.4 | async-start | bytes 3932160 | tf_op jit(solution)/shard_map/all_gather | solution.py:116
  9.4 368.2 %reduce-scatter.3.cloned.1.call-start = ((), (), s32[]{:S(2)}) async-start(), calls=%async_computation.5 | async-start | bytes 3932160 | tf_op jit(solution)/shard_map/reduce_scatter | solution.py:125
  293.3 1.1 copy-start.2
  318.4 122.3 %reduce-scatter.5.cloned.1.call-start = ((), (), s32[]{:S(2)}) async-start(), calls=%async_computation.6 | async-start | bytes 3932160 | tf_op jit(solution)/shard_map/reduce_scatter | solution.py:131
  339.4 113.9 %copy-start.1 = (s32[1,8]{1,0:T(1,128)S(1)}, s32[1,8]{1,0:T(1,128)}, u32[]{:S(2)}) copy-start(s32[1,8]{1,0:T(1,128)} %param.15) | copy-start | bytes 100
  342.5 1.4 copy-start.3
Sparse Core Ops, SparseCore 0:
  9.5 46.1 all-gather.5
  57.3 63.4 all-gather.3
  122.4 62.0 all-gather.7
  318.6 59.0 reduce-scatter.2
  380.4 60.3 reduce-scatter.4
where the time goes:
time: 463 us; the launch traced here: 460 us
  waiting for transfers between devices  258 us (56%)
  matrix products  108 us (23%)
  local copies, waits for them, and re-layouts  58.6 us (13%)
  between operations  13.9 us (3%)
  blocking collectives  10.6 us (2%)
  other arithmetic  9.63 us (2%)
    reduce_scatter x1, waiting for transfers between devices, per_device(): lax.psum_scatter(value_grad_buf.reshape(1, buf_rows, feat_width).astype(j...  61.6 us
    all_gather x1, waiting for transfers between devices, per_device(): lax.all_gather(key_states, 'seq', axis=1, tiled=True)  59.1 us
    all_gather x1, waiting for transfers between devices, per_device(): lax.all_gather(value_states, 'seq', axis=1, tiled=True)  58.1 us
    all_gather x1, waiting for transfers between devices, per_device(): lax.all_gather(output_grad, 'head', axis=2, tiled=True)[0]  44.6 us
    reduce_scatter x1, waiting for transfers between devices, per_device(): lax.psum_scatter(key_grad_buf.reshape(1, buf_rows, feat_width).astype(jnp...  32.6 us
    dot_general x6, matrix products, head_step(): jnp.einsum('iqk,iqe->ike', dscore, query_head, preferred_element_type=jnp...  20.2 us
    dot_general x6, matrix products, head_step(): jnp.einsum('iqk,iqe->ike', weights_b, grad_head, preferred_element_type=j...  16 us
    dot_general x6, matrix products, head_step(): jnp.einsum('iqe,ike->iqk', grad_head, value_head, preferred_element_type=...  13.7 us
  transfers between devices with their start and end apart: 5, of which 5 were waited for; matrix products, arithmetic and copies ran while one was open for 9% of the time, Pallas kernels for 0%

commit v1 on v0

--- a/solution.py
+++ b/solution.py
@@ -1,13 +1,372 @@
+import functools
+import math
+
 import jax
 import jax.numpy as jnp
 from jax import lax
+from jax.experimental import pallas as pl
+from jax.experimental.pallas import tpu as pltpu
 from jax.sharding import PartitionSpec as P
 
 HD = 128
 TILE = 256
-
-
-def attend(query_tiles, key_buf, value_buf, grad_tiles, buf_slots, counts):
+STAT_ROWS = 16
+SMEM = pl.BlockSpec(memory_space=pltpu.SMEM)
+VMEM = pl.BlockSpec(memory_space=pltpu.VMEM)
+ANY = pl.BlockSpec(memory_space=pl.ANY)
+NT = (((1,), (1,)), ((), ()))
+NN = (((1,), (0,)), ((), ()))
+
+
+def mm(lhs, rhs, dims):
+    return lax.dot_general(lhs, rhs, dims, preferred_element_type=jnp.float32)
+
+
+def pack_kernel(heads_ref, q_ref, k_ref, v_ref, *outs):
+    for slot, out in enumerate(outs):
+        cols = pl.ds(pl.multiple_of(heads_ref[slot] * HD, HD), HD)
+        out[0] = q_ref[:, cols]
+        out[1] = k_ref[:, cols]
+        out[2] = v_ref[:, cols]
+
+
+def pack(heads, query, key, value):
+    rows = query.shape[0]
+    slots = heads.shape[0]
+    return pl.pallas_call(
+        pack_kernel,
+        out_shape=[jax.ShapeDtypeStruct((3, rows, HD), query.dtype)] * slots,
+        in_specs=[SMEM, VMEM, VMEM, VMEM],
+        out_specs=[VMEM] * slots,
+        cost_estimate=pl.CostEstimate(
+            flops=0, transcendentals=0, bytes_accessed=6 * (query.size + slots * rows * HD)
+        ),
+        name="pack_heads",
+    )(heads, query, key, value)
+
+
+def project_kernel(has_acc, slots, heads_ref, src_ref, *refs):
+    refs = list(refs)
+    grad_ref, w_even, w_odd = refs[:3]
+    weights = jnp.concatenate([w_even[...], w_odd[...]], axis=0)
+    total = mm(grad_ref[...], weights, NT)
+    if has_acc:
+        total = total + refs[3][0]
+        outs = refs[4:]
+        for slot in range(slots):
+            @pl.when(pl.program_id(0) == slot // 2)
+            def _():
+                half = slot % 2
+                outs[slot][...] = total[:, half * HD : (half + 1) * HD].astype(jnp.bfloat16)
+    else:
+        refs[3][0] = total
+
+
+def project(heads, src, grads, w_out, acc, last):
+    rows, feats = grads.shape
+    slots = heads.shape[0]
+    steps = slots // 2
+    in_specs = [
+        pl.BlockSpec((rows, feats), lambda s, heads, src: (0, 0)),
+        pl.BlockSpec((HD, feats), lambda s, heads, src: (heads[2 * s], src[0])),
+        pl.BlockSpec((HD, feats), lambda s, heads, src: (heads[2 * s + 1], src[0])),
+    ]
+    args = [grads, w_out, w_out]
+    acc_spec = pl.BlockSpec((1, rows, 2 * HD), lambda s, heads, src: (s, 0, 0))
+    if acc is not None:
+        in_specs.append(acc_spec)
+        args.append(acc)
+    if last:
+        out_shape = [jax.ShapeDtypeStruct((rows, HD), jnp.bfloat16)] * slots
+        out_specs = [pl.BlockSpec((rows, HD), lambda s, heads, src: (0, 0))] * slots
+    else:
+        out_shape = jax.ShapeDtypeStruct((steps, rows, 2 * HD), jnp.float32)
+        out_specs = acc_spec
+    return pl.pallas_call(
+        functools.partial(project_kernel, last, slots),
+        out_shape=out_shape,
+        grid_spec=pltpu.PrefetchScalarGridSpec(
+            num_scalar_prefetch=2, grid=(steps,), in_specs=in_specs, out_specs=out_specs
+        ),
+        cost_estimate=pl.CostEstimate(
+            flops=2 * rows * feats * slots * HD,
+            transcendentals=0,
+            bytes_accessed=2 * (grads.size + slots * HD * feats) + 6 * slots * rows * HD,
+        ),
+        name="project_last" if last else "project_own",
+    )(heads, src, *args)
+
+
+def attend_kernel(parts, tiles_dev, me_ref, mask_ref, *refs):
+    tiles = parts * tiles_dev
+    qkv_refs = refs[:parts]
+    grad_refs = refs[parts : 2 * parts]
+    outs = refs[2 * parts : 3 * parts]
+    q_s, k_s, v_s, g_s, kt_s, dk_s, dv_s, dq_s, e_s, dp_s, dqt_s, m_s, l_s, d_s = refs[3 * parts :]
+    score_scale = HD ** (-0.5)
+    expo = score_scale * math.log2(math.e)
+    me = me_ref[0]
+    for part in range(parts):
+        for sub in range(tiles_dev):
+            tile = part * tiles_dev + sub
+            span = slice(sub * TILE, (sub + 1) * TILE)
+            q_s[tile] = qkv_refs[part][0, span, :]
+            key = qkv_refs[part][1, span, :]
+            k_s[tile] = key
+            kt_s[tile] = key.T
+            v_s[tile] = qkv_refs[part][2, span, :]
+            g_s[tile] = grad_refs[part][span, :]
+    dk_s[...] = jnp.zeros_like(dk_s)
+    dv_s[...] = jnp.zeros_like(dv_s)
+
+    def place(tile):
+        part = lax.div(tile, tiles_dev)
+        return lax.rem(me - part + parts, parts) * tiles_dev + lax.rem(tile, tiles_dev)
+
+    key_place = [
+        lax.rem(me - tile // tiles_dev + parts, parts) * tiles_dev + tile % tiles_dev
+        for tile in range(tiles)
+    ]
+
+    def query_step(qi, query_sq):
+        own = place(qi)
+        query = q_s[qi]
+        grad = g_s[qi]
+        m_s[...] = jnp.full_like(m_s, -jnp.inf)
+        l_s[...] = jnp.zeros_like(l_s)
+        d_s[...] = jnp.zeros_like(d_s)
+        dqt_s[...] = jnp.zeros_like(dqt_s)
+        for ki in range(tiles):
+            @pl.when(mask_ref[own, key_place[ki]] != 0)
+            def _(ki=ki):
+                scores = mm(k_s[ki], query, NT)
+                dprob = mm(v_s[ki], grad, NT)
+                top = jnp.max(scores, axis=0, keepdims=True)
+                weight = jnp.exp2((scores - top) * expo)
+                m_s[ki : ki + 1, :] = top
+                l_s[ki : ki + 1, :] = jnp.sum(weight, axis=0, keepdims=True)
+                d_s[ki : ki + 1, :] = jnp.sum(weight * dprob, axis=0, keepdims=True)
+                e_s[ki] = weight
+                dp_s[ki] = dprob
+
+        tops = m_s[...]
+        factor = jnp.exp2((tops - jnp.max(tops, axis=0, keepdims=True)) * expo)
+        norm = jnp.sum(l_s[...] * factor, axis=0, keepdims=True)
+        delta = jnp.sum(d_s[...] * factor, axis=0, keepdims=True) / norm
+        m_s[...] = factor / norm
+        for ki in range(tiles):
+            @pl.when(mask_ref[own, key_place[ki]] != 0)
+            def _(ki=ki):
+                weight = e_s[ki] * m_s[ki : ki + 1, :]
+                dscore = (weight * (dp_s[ki] - delta)).astype(jnp.bfloat16)
+                dv_s[ki] += mm(weight.astype(jnp.bfloat16), grad, NN)
+                dk_s[ki] += mm(dscore, query, NN)
+                dqt_s[...] += mm(kt_s[ki], dscore, NN)
+
+        query_full = dqt_s[...].T * score_scale
+        dq_s[qi] = query_full.astype(jnp.bfloat16)
+        return query_sq + jnp.sum(query_full * query_full, axis=0, keepdims=True)
+
+    query_sq = lax.fori_loop(0, tiles, query_step, jnp.zeros((1, HD), jnp.float32))
+    key_sq = jnp.zeros((1, HD), jnp.float32)
+    value_sq = jnp.zeros((1, HD), jnp.float32)
+    rows = tiles_dev * TILE
+    for part in range(parts):
+        for sub in range(tiles_dev):
+            tile = part * tiles_dev + sub
+            key_full = dk_s[tile] * score_scale
+            value_full = dv_s[tile]
+            key_sq = key_sq + jnp.sum(key_full * key_full, axis=0, keepdims=True)
+            value_sq = value_sq + jnp.sum(value_full * value_full, axis=0, keepdims=True)
+            low = sub * TILE
+            outs[part][low : low + TILE, :] = dq_s[tile]
+            outs[part][rows + low : rows + low + TILE, :] = key_full.astype(jnp.bfloat16)
+            outs[part][2 * rows + low : 2 * rows + low + TILE, :] = value_full.astype(jnp.bfloat16)
+    row = lax.broadcasted_iota(jnp.int32, (STAT_ROWS, HD), 0)
+    total = jnp.where(
+        row < 3,
+        jnp.sum(query_sq, axis=1, keepdims=True),
+        jnp.where(
+            row < 6,
+            jnp.sum(key_sq, axis=1, keepdims=True),
+            jnp.sum(value_sq, axis=1, keepdims=True),
+        ),
+    )
+    high = total.astype(jnp.bfloat16).astype(jnp.float32)
+    mid = (total - high).astype(jnp.bfloat16).astype(jnp.float32)
+    low = total - high - mid
+    piece = lax.rem(row, 3)
+    stats = jnp.where(piece == 0, high, jnp.where(piece == 1, mid, low)).astype(jnp.bfloat16)
+    for part in range(parts):
+        outs[part][3 * rows :, :] = stats
+
+
+def attend(me, mask, qkv, grads):
+    parts = len(qkv)
+    rows = qkv[0].shape[1]
+    tiles_dev = rows // TILE
+    tiles = parts * tiles_dev
+    bf16, f32 = jnp.bfloat16, jnp.float32
+    pairs = tiles * tiles
+    return pl.pallas_call(
+        functools.partial(attend_kernel, parts, tiles_dev),
+        out_shape=[jax.ShapeDtypeStruct((3 * rows + STAT_ROWS, HD), bf16)] * parts,
+        in_specs=[SMEM, SMEM] + [VMEM] * (2 * parts),
+        out_specs=[VMEM] * parts,
+        scratch_shapes=[
+            pltpu.VMEM((tiles, TILE, HD), bf16),
+            pltpu.VMEM((tiles, TILE, HD), bf16),
+            pltpu.VMEM((tiles, TILE, HD), bf16),
+            pltpu.VMEM((tiles, TILE, HD), bf16),
+            pltpu.VMEM((tiles, HD, TILE), bf16),
+            pltpu.VMEM((tiles, TILE, HD), f32),
+            pltpu.VMEM((tiles, TILE, HD), f32),
+            pltpu.VMEM((tiles, TILE, HD), bf16),
+            pltpu.VMEM((tiles, TILE, TILE), f32),
+            pltpu.VMEM((tiles, TILE, TILE), f32),
+            pltpu.VMEM((HD, TILE), f32),
+            pltpu.VMEM((tiles, TILE), f32),
+            pltpu.VMEM((tiles, TILE), f32),
+            pltpu.VMEM((tiles, TILE), f32),
+        ],
+        cost_estimate=pl.CostEstimate(
+            flops=pairs * 10 * TILE * TILE * HD,
+            transcendentals=pairs * TILE * TILE,
+            bytes_accessed=2 * 7 * parts * rows * HD,
+        ),
+        name="attend_head",
+    )(me, mask, *qkv, *grads)
+
+
+def unpack_kernel(parts, rows, count, fresh, heads_ref, live_ref, *refs):
+    blocks = refs[:parts]
+    rest = refs[parts:]
+    feats = None
+    if not fresh:
+        feats = rest[3][...]
+        rest = rest[4:]
+    outs = rest[:3]
+    feat_out = rest[3]
+    sems = rest[4]
+    if fresh:
+        feats = jnp.zeros(feat_out.shape, jnp.float32)
+
+    def copies(slot):
+        cols = pl.ds(pl.multiple_of(heads_ref[slot] * HD, HD), HD)
+        return [
+            pltpu.make_async_copy(
+                blocks[slot].at[pl.ds(j * rows, rows), :], outs[j].at[:, cols], sems.at[slot, j]
+            )
+            for j in range(3)
+        ]
+
+    for slot in range(parts):
+        @pl.when(live_ref[slot] != 0)
+        def _():
+            for copy in copies(slot):
+                copy.start()
+
+    row = lax.broadcasted_iota(jnp.int32, feat_out.shape, 0)
+    col = lax.broadcasted_iota(jnp.int32, feat_out.shape, 1)
+    for slot in range(parts):
+        stats = blocks[slot][3 * rows :, :].astype(jnp.float32)
+        here = (row == heads_ref[slot]) & (live_ref[slot] != 0)
+        for j in range(3):
+            total = stats[3 * j : 3 * j + 1, :3] + stats[3 * j + 1 : 3 * j + 2, :3]
+            total = total + stats[3 * j + 2 : 3 * j + 3, :3]
+            feats = jnp.where(here & (col == j), jnp.log(total / count + 1e-06), feats)
+    feat_out[...] = feats
+    for slot in range(parts):
+        @pl.when(live_ref[slot] != 0)
+        def _():
+            for copy in copies(slot):
+                copy.wait()
+
+
+def unpack(heads, live, blocks, before, head_count, count):
+    parts = len(blocks)
+    rows = (blocks[0].shape[0] - STAT_ROWS) // 3
+    fresh = before is None
+    kept = [] if fresh else list(before)
+    big = jax.ShapeDtypeStruct((rows, head_count * HD), jnp.bfloat16)
+    return pl.pallas_call(
+        functools.partial(unpack_kernel, parts, rows, count, fresh),
+        out_shape=[big, big, big, jax.ShapeDtypeStruct((head_count, 3), jnp.float32)],
+        in_specs=[SMEM, SMEM] + [VMEM] * parts + ([] if fresh else [ANY, ANY, ANY, VMEM]),
+        out_specs=[ANY, ANY, ANY, VMEM],
+        scratch_shapes=[pltpu.SemaphoreType.DMA((parts, 3))],
+        input_output_aliases={} if fresh else {2 + parts + j: j for j in range(3)},
+        cost_estimate=pl.CostEstimate(
+            flops=0, transcendentals=0, bytes_accessed=12 * parts * rows * HD
+        ),
+        name="unpack_heads",
+    )(heads, live, *blocks, *kept)
+
+
+def shift(arr, axis, step, size, targets):
+    pairs = [(s, (s + step) % size) for s in range(size) if (s + step) % size in targets]
+    return lax.ppermute(arr, axis, pairs)
+
+
+def shift_back(arr, axis, step, size, sources):
+    return lax.ppermute(arr, axis, [(s, (s - step) % size) for s in sources])
+
+
+def allowed_tiles(key_list, key_count):
+    tiles, slots = key_list.shape
+    live = jnp.arange(slots)[None, :] < key_count[:, None]
+    hit = (key_list[:, :, None] == jnp.arange(tiles)[None, None, :]) & live[:, :, None]
+    return jnp.any(hit, axis=1).astype(jnp.int32)
+
+
+def by_heads(query_states, key_states, value_states, output_grad, w_out, key_list, key_count):
+    parts = lax.axis_size("seq")
+    me = lax.axis_index("seq")
+    sides = lax.axis_size("head")
+    side = lax.axis_index("head")
+    rows, width = query_states.shape[1:]
+    head_count = width // HD
+    full, extra = divmod(head_count, parts)
+    low = (parts - extra) // 2
+    rounds = [(k * parts, 0, parts) for k in range(full)]
+    if extra:
+        rounds.append((full * parts, low, extra))
+    dest = lax.rem(me + jnp.arange(parts, dtype=jnp.int32), parts)
+    heads, lives, targets = [], [], []
+    for base, first, size in rounds:
+        heads.append(base + jnp.clip(dest - first, 0, size - 1).astype(jnp.int32))
+        lives.append(((dest >= first) & (dest < first + size)).astype(jnp.int32))
+        targets.append(list(range(first, first + size)))
+    me_arr = me.astype(jnp.int32).reshape(1)
+    mask = allowed_tiles(key_list[0], key_count[0])
+    other = [
+        lax.ppermute(output_grad[0], "head", [(s, (s + i) % sides) for s in range(sides)])
+        for i in range(1, sides)
+    ]
+    qkv = []
+    for head, target in zip(heads, targets):
+        slots = pack(head, query_states[0], key_states[0], value_states[0])
+        qkv.append(
+            [slots[0]] + [shift(slots[i], "seq", i, parts, target) for i in range(1, parts)]
+        )
+    all_heads = jnp.concatenate(heads)
+    acc = project(all_heads, side.astype(jnp.int32).reshape(1), output_grad[0], w_out, None, False)
+    for i in range(1, sides):
+        src = lax.rem(side - i + sides, sides).astype(jnp.int32).reshape(1)
+        acc = project(all_heads, src, other[i - 1], w_out, acc, i == sides - 1)
+    before = None
+    for k, (head, live, target) in enumerate(zip(heads, lives, targets)):
+        slots = acc[k * parts : (k + 1) * parts]
+        grads = [slots[0]] + [shift(slots[i], "seq", i, parts, target) for i in range(1, parts)]
+        done = attend(me_arr, mask * live[0], qkv[k], grads)
+        back = [done[0]] + [
+            shift_back(done[i], "seq", i, parts, target) for i in range(1, parts)
+        ]
+        before = unpack(head, live, back, before, head_count, parts * rows * HD)
+    return tuple(arr[None] for arr in before)
+
+
+def attend_gathered(query_tiles, key_buf, value_buf, grad_tiles, buf_slots, counts):
     score_scale = HD ** (-0.5)
     tile_count, tile_rows, feat_width = query_tiles.shape
     slot_count = buf_slots.shape[1]
@@ -93,7 +452,7 @@
     return jnp.sum(rows * rows, axis=(0, 2))
 
 
-def per_device(query_states, key_states, value_states, output_grad, w_out, key_list, key_count):
+def by_gather(query_states, key_states, value_states, output_grad, w_out, key_list, key_count):
     seq_count = lax.axis_size("seq")
     seq_index = lax.axis_index("seq")
     tok_rows = query_states.shape[1]
@@ -117,7 +476,7 @@
     )
     key_buf = key_whole[0].reshape(-1, TILE, feat_width)
     value_buf = value_whole[0].reshape(-1, TILE, feat_width)
-    query_full, key_grad_buf, value_grad_buf = attend(
+    query_full, key_grad_buf, value_grad_buf = attend_gathered(
         query_tiles, key_buf, value_buf, grad_tiles, own_lists, own_counts
     )
     buf_rows = key_grad_buf.shape[0] * TILE
@@ -156,6 +515,14 @@
     )
 
 
+def per_device(*args):
+    parts, sides = lax.axis_size("seq"), lax.axis_size("head")
+    head_count = args[0].shape[2] // HD
+    if head_count >= parts > 1 and parts % 2 == 0 and sides > 1:
+        return by_heads(*args)
+    return by_gather(*args)
+
+
 def solution(mesh):
     in_specs = (
         P(("grp", "clip"), "seq", "head"),

time: 463 us -> 178 us (0.38)
  waiting for transfers between devices: 258 us -> 52.4 us
  matrix products: 108 us -> 0 us
  Pallas kernels: 0 us -> 68.2 us
  local copies, waits for them, and re-layouts: 58.6 us -> 4.98 us
  starting transfers between devices: 0.19 us -> 48 us
  between operations: 13.9 us -> 0.92 us
  blocking collectives: 10.6 us -> 0 us
  other arithmetic: 9.63 us -> 2.07 us
    all_gather x3 -> x0, waiting for transfers between devices: 162 us -> none  [the longest x1 59.1 us: per_device(): lax.all_gather(key_states, 'seq', axis=1, tiled=True)]
    dot_general x39 -> x0, matrix products: 108 us -> none  [the longest x6 20.2 us: head_step(): jnp.einsum('iqk,iqe->ike', dscore, query_head, preferred_element_type=jnp...]
    reduce_scatter x2 -> x0, waiting for transfers between devices: 94.2 us -> none  [the longest x1 61.6 us: per_device(): lax.psum_scatter(value_grad_buf.reshape(1, buf_rows, feat_width).astype(j...]
    pallas_call x0 -> x8, Pallas kernels: none -> 68.2 us  [the longest x2 42.3 us: attend(): pl.pallas_call(functools.partial(attend_kernel, parts, tiles_dev), out_sh...]
    ppermute x0 -> x19, waiting for transfers between devices: none -> 52.4 us  [the longest x6 39.8 us: shift_back(): return lax.ppermute(arr, axis, [(s, (s - step) % size) for s in sources])]
    ppermute x0 -> x19, starting transfers between devices: none -> 48 us  [the longest x12 38.4 us: shift(): return lax.ppermute(arr, axis, pairs)]
    reshape x2 -> x0, local copies, waits for them, and re-layouts: 26.6 us -> none  [the longest x1 13.3 us: attend(): value_sel_grad.reshape(tile_count, slot_count, tile_rows * feat_width)]
    gather x2 -> x0, local copies, waits for them, and re-layouts: 11.1 us -> none  [the longest x1 5.55 us: attend(): key_sel = key_buf[buf_slots].reshape(tile_count, key_span, feat_width)]
  transfers between devices with their start and end apart: 5 -> 19, of which waited for: 5 -> 4; matrix products, arithmetic and copies ran while one was open for 9% -> 1% of each run, Pallas kernels for 0% -> 37%
where the time goes in v1:
time: 178 us; the launch traced here: 177 us
  Pallas kernels  68.2 us (38%)
  waiting for transfers between devices  52.4 us (29%)
  starting transfers between devices  48 us (27%)
  local copies, waits for them, and re-layouts  4.98 us (3%)
  other arithmetic  2.07 us (1%)
    pallas_call x2, Pallas kernels, attend(): pl.pallas_call(functools.partial(attend_kernel, parts, tiles_dev), out_sh...  42.3 us
    ppermute x6, waiting for transfers between devices, shift_back(): return lax.ppermute(arr, axis, [(s, (s - step) % size) for s in sources])  39.8 us
    ppermute x12, starting transfers between devices, shift(): return lax.ppermute(arr, axis, pairs)  38.4 us
    pallas_call x2, Pallas kernels, project(): pl.pallas_call(functools.partial(project_kernel, last, slots), out_shape=...  13.7 us
    ppermute x1, waiting for transfers between devices, by_heads(): lax.ppermute(output_grad[0], 'head', [(s, (s + i) % sides) for s in range...  12.6 us
    ppermute x6, starting transfers between devices, shift_back(): return lax.ppermute(arr, axis, [(s, (s - step) % size) for s in sources])  8.11 us
    pallas_call x2, Pallas kernels, unpack(): pl.pallas_call(functools.partial(unpack_kernel, parts, rows, count, fresh...  6.13 us
    pallas_call x2, Pallas kernels, pack(): pl.pallas_call(pack_kernel, out_shape=[jax.ShapeDtypeStruct((3, rows, HD)...  6.08 us
  transfers between devices with their start and end apart: 19, of which 4 were waited for; matrix products, arithmetic and copies ran while one was open for 1% of the time, Pallas kernels for 37%

profile of v1, /device:TPU:4, one launch (start us, length us, event | category | flops | bytes accessed | tf_op | source)
XLA Modules:
  0.0 176.7 jit_solution(17011622559176392712)
XLA Ops:
  0.6 1.6 collective-permute-start.3
  2.2 0.6 clamp_add_fusion
  2.8 3.1 %pack_heads.3 = (bf16[3,512,128]{2,1,0:T(8,128)(2,1)}, bf16[3,512,128]{2,1,0:T(8,128)(2,1)}, bf16[3,512,128]{2,1,0:T(8,128)(2,1)}, bf16[3,512,128]{2,1,0:T(8,128)(2,1)}) custom-call(s32[4]{0:T(128)} %get-tuple-element.79.heads_ref, bf16[512,768]{1,0:T(8,128)(2,1)} %bitcast.17, bf16[512,768]{1,0:T(8,128)(2,1)} %bitcast.19, bf16[512,768]{1,0:T(8,128)(2,1)} %bitcast.21), custom_call_target="tpu_custom_call" | custom-call | bytes 3932160 | tf_op jit(solution)/shard_map/pack_heads/pallas_call | solution.py:36
  5.8 1.6 collective-permute-start.10
  7.4 2.6 %collective-permute-start.11 = (bf16[3,512,128]{2,1,0:T(8,128)(2,1)}, bf16[3,512,128]{2,1,0:T(8,128)(2,1)S(1)}, u32[]{:S(2)}, u32[]{:S(2)}) collective-permute-start(bf16[3,512,128]{2,1,0:T(8,128)(2,1)} %get-tuple-element.50), channel_id=1, source_target_pairs={{0,8},{4,12},{8,0},{12,4},{1,9},{5,13},{9,1},{13,5},{2,10},{6,14},... | collective-permute-start | bytes 1179656 | tf_op jit(solution)/shard_map/ppermute | solution.py:308
  10.0 1.3 collective-permute-start.12
  11.4 3.0 %pack_heads.2 = (bf16[3,512,128]{2,1,0:T(8,128)(2,1)}, bf16[3,512,128]{2,1,0:T(8,128)(2,1)}, bf16[3,512,128]{2,1,0:T(8,128)(2,1)}, bf16[3,512,128]{2,1,0:T(8,128)(2,1)}) custom-call(s32[4]{0:T(128)} %get-tuple-element.78.heads_ref, bf16[512,768]{1,0:T(8,128)(2,1)} %bitcast.18, bf16[512,768]{1,0:T(8,128)(2,1)} %bitcast.20, bf16[512,768]{1,0:T(8,128)(2,1)} %bitcast.22), custom_call_target="tpu_custom_call" | custom-call | bytes 3932160 | tf_op jit(solution)/shard_map/pack_heads/pallas_call | solution.py:36
  14.4 2.6 %collective-permute-start = (bf16[3,512,128]{2,1,0:T(8,128)(2,1)}, bf16[3,512,128]{2,1,0:T(8,128)(2,1)S(1)}, u32[]{:S(2)}, u32[]{:S(2)}) collective-permute-start(bf16[3,512,128]{2,1,0:T(8,128)(2,1)} %get-tuple-element.37), channel_id=1, source_target_pairs={{0,4},{4,8},{1,5},{5,9},{2,6},{6,10},{3,7},{7,11},{16,20},{20,24},... | collective-permute-start | bytes 1179656 | tf_op jit(solution)/shard_map/ppermute | solution.py:308
  17.0 0.7 pad_add_fusion.heads_ref
  17.7 6.6 %project_own.1.refs_3_ = f32[4,512,256]{2,1,0:T(8,128)} custom-call(s32[8]{0:T(128)} %pad_add_fusion.heads_ref, s32[1]{0:T(128)} %bitcast.9.src_ref, bf16[512,1536]{1,0:T(8,128)(2,1)} %bitcast.24, bf16[768,3072]{1,0:T(8,128)(2,1)} %refs_2_.3, bf16[768,3072]{1,0:T(8,128)(2,1)} %refs_2_.3), custom_call_target="tpu_custom_call" | custom-call | flops 1610612736 | bytes 7864320 | tf_op jit(solution)/shard_map/project_own/pallas_call | solution.py:85
  24.2 0.0 copy-done.23
  24.2 0.1 iota_compare_fusion.1
  24.3 0.1 fusion.1
  24.5 0.0 copy-start.10
  24.5 12.6 %collective-permute-done.3.refs_0_ = bf16[512,1536]{1,0:T(8,128)(2,1)S(1)} collective-permute-done((bf16[512,1536]{1,0:T(8,128)(2,1)}, bf16[512,1536]{1,0:T(8,128)(2,1)S(1)}, u32[]{:S(2)}, u32[]{:S(2)}) %collective-permute-start.3) | collective-permute-done | bytes 1572896 | tf_op jit(solution)/shard_map/ppermute | solution.py:343
  37.0 1.2 copy-done
  38.2 7.2 %project_last.1 = (bf16[512,128]{1,0:T(8,128)(2,1)}, bf16[512,128]{1,0:T(8,128)(2,1)}, bf16[512,128]{1,0:T(8,128)(2,1)}, bf16[512,128]{1,0:T(8,128)(2,1)}, bf16[...) custom-call(s32[8]{0:T(128)} %pad_add_fusion.heads_ref, ...), custom_call_target="tpu_custom_call" | custom-call | flops 1610612736 | bytes 7864320 | tf_op jit(solution)/shard_map/project_last/pallas_call | solution.py:85
  45.4 1.6 collective-permute-start.13
  47.0 0.0 collective-permute-done.10.refs_1_
  47.0 2.6 %collective-permute-start.14 = (bf16[512,128]{1,0:T(8,128)(2,1)}, bf16[512,128]{1,0:T(8,128)(2,1)S(1)}, u32[]{:S(2)}, u32[]{:S(2)}) collective-permute-start(bf16[512,128]{1,0:T(8,128)(2,1)} %get-tuple-element.54), channel_id=1, source_target_pairs={{0,8},{4,12},{8,0},{12,4},{1,9},{5,13},{9,1},{13,5},{2,10},{6,14},... | collective-permute-start | bytes 393224 | tf_op jit(solution)/shard_map/ppermute | solution.py:308
  49.5 0.0 collective-permute-done.11.refs_2_
  49.5 1.4 collective-permute-start.15
  50.9 0.6 broadcast_select_fusion
  51.5 0.0 collective-permute-done.12.refs_3_
  51.5 2.2 %collective-permute-start.1 = (bf16[3,512,128]{2,1,0:T(8,128)(2,1)S(1)}, bf16[3,512,128]{2,1,0:T(8,128)(2,1)S(1)}, u32[]{:S(2)}, u32[]{:S(2)}) collective-permute-start(bf16[3,512,128]{2,1,0:T(8,128)(2,1)S(1)} %copy-done.16), channel_id=1, source_target_pairs={{0,8},{12,4},{1,9},{13,5},{2,10},{14,6},{3,11},{15,7},{16,24},{28,... | collective-permute-start | bytes 1179656 | tf_op jit(solution)/shard_map/ppermute | solution.py:308
  53.8 0.0 collective-permute-done.refs_1_
  53.8 0.7 collective-permute-start.2
  54.5 0.0 collective-permute-done.13.refs_5_
  54.5 16.7 %collective-permute-start.4 = (bf16[512,128]{1,0:T(8,128)(2,1)}, bf16[512,128]{1,0:T(8,128)(2,1)S(1)}, u32[]{:S(2)}, u32[]{:S(2)}) collective-permute-start(bf16[512,128]{1,0:T(8,128)(2,1)} %get-tuple-element.41), channel_id=1, source_target_pairs={{0,4},{4,8},{1,5},{5,9},{2,6},{6,10},{3,7},{7,11},{16,20},{20,24},... | collective-permute-start | bytes 393224 | tf_op jit(solution)/shard_map/ppermute | solution.py:308
  71.3 0.0 collective-permute-done.14.refs_6_
  71.3 3.8 %collective-permute-start.5 = (bf16[512,128]{1,0:T(8,128)(2,1)}, bf16[512,128]{1,0:T(8,128)(2,1)}, u32[]{:S(2)}, u32[]{:S(2)}) collective-permute-start(bf16[512,128]{1,0:T(8,128)(2,1)} %get-tuple-element.42), channel_id=1, source_target_pairs={{0,8},{12,4},{1,9},{13,5},{2,10},{14,6},{3,11},{15,7},{16,24},{28,... | collective-permute-start | bytes 393224 | tf_op jit(solution)/shard_map/ppermute | solution.py:308
  75.1 0.0 collective-permute-done.15.refs_7_
  75.1 1.3 collective-permute-start.6
  76.4 0.0 copy-done.14
  76.4 0.0 copy-done.22
  76.4 36.5 %attend_head.3 = (bf16[1552,128]{1,0:T(8,128)(2,1)}, bf16[1552,128]{1,0:T(8,128)(2,1)}, bf16[1552,128]{1,0:T(8,128)(2,1)}, bf16[1552,128]{1,0:T(8,128)(2,1)}) custom-call(s32[1]{0:T(128)} %bitcast.me_ref, s32[8,8]{1,0:T(8,128)} %get-tuple-element.76.mask_ref, bf16[3,512,128]{2,1,0:T(8,128)(2,1)} %get-tuple-element.48.refs_0_, ...), custom_call_target="tpu_custom_call" | custom-call | flops 5368709120 | bytes 3670016 | tf_op jit(solution)/shard_map/attend_head/pallas_call | solution.py:211
  112.9 0.0 copy-done.12
  112.9 0.0 collective-permute-done.1.refs_2_
  112.9 0.0 copy-start.17
  112.9 4.3 %collective-permute-start.16 = (bf16[1552,128]{1,0:T(8,128)(2,1)}, bf16[1552,128]{1,0:T(8,128)(2,1)S(1)}, u32[]{:S(2)}, u32[]{:S(2)}) collective-permute-start(bf16[1552,128]{1,0:T(8,128)(2,1)} %get-tuple-element.57), channel_id=1, source_target_pairs={{0,12},{4,0},{8,4},{12,8},{1,13},{5,1},{9,5},{13,9},{2,14},{6,2},{... | collective-permute-start | bytes 1191944 | tf_op jit(solution)/shard_map/ppermute | solution.py:312
  117.2 0.0 collective-permute-done.2.refs_3_
  117.2 0.0 collective-permute-start.17
  117.2 0.0 collective-permute-done.4.refs_5_
  117.2 0.7 copy-done.19
  117.9 0.6 collective-permute-start.18
  118.5 0.0 collective-permute-done.5.refs_6_
  118.5 0.0 collective-permute-done.6.refs_7_
  118.5 5.8 %attend_head.2 = (bf16[1552,128]{1,0:T(8,128)(2,1)}, bf16[1552,128]{1,0:T(8,128)(2,1)}, bf16[1552,128]{1,0:T(8,128)(2,1)}, bf16[1552,128]{1,0:T(8,128)(2,1)}) custom-call(s32[1]{0:T(128)} %bitcast.me_ref, s32[8,8]{1,0:T(8,128)} %get-tuple-element.77.mask_ref, bf16[3,512,128]{2,1,0:T(8,128)(2,1)} %get-tuple-element.36.refs_0_, ...), custom_call_target="tpu_custom_call" | custom-call | flops 5368709120 | bytes 3670016 | tf_op jit(solution)/shard_map/attend_head/pallas_call | solution.py:211
  124.3 1.3 collective-permute-start.7
  125.6 1.3 collective-permute-start.8
  126.9 0.0 collective-permute-done.16.refs_1_
  126.9 0.7 collective-permute-start.9
  127.6 10.7 %collective-permute-done.17.refs_2_ = bf16[1552,128]{1,0:T(8,128)(2,1)S(1)} collective-permute-done((bf16[1552,128]{1,0:T(8,128)(2,1)}, bf16[1552,128]{1,0:T(8,128)(2,1)S(1)}, u32[]{:S(2)}, u32[]{:S(2)}) %collective-permute-start.17) | collective-permute-done | bytes 397344 | tf_op jit(solution)/shard_map/ppermute | solution.py:312
  138.4 0.0 collective-permute-done.18.refs_3_
  138.4 0.7 copy-done.5
  139.1 0.1 copy-done.6
  139.3 3.2 %unpack_heads.2 = (bf16[512,768]{1,0:T(8,128)(2,1)}, bf16[512,768]{1,0:T(8,128)(2,1)}, bf16[512,768]{1,0:T(8,128)(2,1)}, f32[6,3]{1,0:T(8,128)}) custom-call(s32[4]{0:T(128)} %get-tuple-element.79.heads_ref, s32[4]{0:T(128)} %copy-done.11, bf16[1552,128]{1,0:T(8,128)(2,1)} %get-tuple-element.56.refs_0_, bf16[1552,128]{1,0:T(8,128)(2,1)} %copy-done.4, ...), custom_call_target="tpu_custom_call" | custom-call | bytes 3145728 | tf_op jit(solution)/shard_map/unpack_heads/pallas_call | solution.py:292
  142.5 23.4 %collective-permute-done.7.refs_1_ = bf16[1552,128]{1,0:T(8,128)(2,1)S(1)} collective-permute-done((bf16[1552,128]{1,0:T(8,128)(2,1)}, bf16[1552,128]{1,0:T(8,128)(2,1)S(1)}, u32[]{:S(2)}, u32[]{:S(2)}) %collective-permute-start.7) | collective-permute-done | bytes 397344 | tf_op jit(solution)/shard_map/ppermute | solution.py:312
  165.8 5.7 %collective-permute-done.8.refs_2_ = bf16[1552,128]{1,0:T(8,128)(2,1)S(1)} collective-permute-done((bf16[1552,128]{1,0:T(8,128)(2,1)}, bf16[1552,128]{1,0:T(8,128)(2,1)S(1)}, u32[]{:S(2)}, u32[]{:S(2)}) %collective-permute-start.8) | collective-permute-done | bytes 397344 | tf_op jit(solution)/shard_map/ppermute | solution.py:312
  171.5 0.0 collective-permute-done.9.refs_3_
  171.6 0.8 copy-done.2
  172.3 0.1 copy-done.3
  172.4 2.9 %unpack_heads.3 = (bf16[512,768]{1,0:T(8,128)(2,1)}, bf16[512,768]{1,0:T(8,128)(2,1)}, bf16[512,768]{1,0:T(8,128)(2,1)}, f32[6,3]{1,0:T(8,128)}) custom-call(s32[4]{0:T(128)} %get-tuple-element.78.heads_ref, s32[4]{0:T(128)} %copy-done.10, bf16[1552,128]{1,0:T(8,128)(2,1)} %get-tuple-element.44.refs_0_, ...), custom_call_target="tpu_custom_call", output_to_operand_aliasing={{0}: (6, {}), {1}: (7, {}), {2}: (8, {})} | custom-call | bytes 3145728 | tf_op jit(solution)/shard_map/unpack_heads/pallas_call | solution.py:292
  175.4 1.3 copy.17
  (38 shorter events, 0.1 us)
Async XLA Ops:
  0.6 36.4 %collective-permute-start.3 = (bf16[512,1536]{1,0:T(8,128)(2,1)}, bf16[512,1536]{1,0:T(8,128)(2,1)S(1)}, u32[]{:S(2)}, u32[]{:S(2)}) collective-permute-start(bf16[512,1536]{1,0:T(8,128)(2,1)} %bitcast.23), channel_id=1, source_target_pairs={{0,2},{2,0},{1,3},{3,1},{4,6},{6,4},{5,7},{7,5},{8,10},{10,8},{9,1... | collective-permute-start | bytes 4718600 | tf_op jit(solution)/shard_map/ppermute | solution.py:343
  2.8 14.2 %copy-start.8 = (s32[4]{0:T(128)S(1)}, s32[4]{0:T(128)}, u32[]{:S(2)}) copy-start(s32[4]{0:T(128)} %get-tuple-element.78.heads_ref) | copy-start | bytes 52
  2.8 14.2 %copy-start.9 = (s32[4]{0:T(128)S(1)}, s32[4]{0:T(128)}, u32[]{:S(2)}) copy-start(s32[4]{0:T(128)} %get-tuple-element.79.heads_ref) | copy-start | bytes 52
  5.8 41.1 %collective-permute-start.10 = (bf16[3,512,128]{2,1,0:T(8,128)(2,1)}, bf16[3,512,128]{2,1,0:T(8,128)(2,1)S(1)}, u32[]{:S(2)}, u32[]{:S(2)}) collective-permute-start(bf16[3,512,128]{2,1,0:T(8,128)(2,1)} %get-tuple-element.49), channel_id=1, source_target_pairs={{0,4},{4,8},{8,12},{12,0},{1,5},{5,9},{9,13},{13,1},{2,6},{6,10},{... | collective-permute-start | bytes 1179656 | tf_op jit(solution)/shard_map/ppermute | solution.py:308
  7.4 42.1 %collective-permute-start.11 = (bf16[3,512,128]{2,1,0:T(8,128)(2,1)}, bf16[3,512,128]{2,1,0:T(8,128)(2,1)S(1)}, u32[]{:S(2)}, u32[]{:S(2)}) collective-permute-start(bf16[3,512,128]{2,1,0:T(8,128)(2,1)} %get-tuple-element.50), channel_id=1, source_target_pairs={{0,8},{4,12},{8,0},{12,4},{1,9},{5,13},{9,1},{13,5},{2,10},{6,14},... | collective-permute-start | bytes 1179656 | tf_op jit(solution)/shard_map/ppermute | solution.py:308
  10.0 41.5 %collective-permute-start.12 = (bf16[3,512,128]{2,1,0:T(8,128)(2,1)}, bf16[3,512,128]{2,1,0:T(8,128)(2,1)}, u32[]{:S(2)}, u32[]{:S(2)}) collective-permute-start(bf16[3,512,128]{2,1,0:T(8,128)(2,1)} %get-tuple-element.51), channel_id=1, source_target_pairs={{0,12},{4,0},{8,4},{12,8},{1,13},{5,1},{9,5},{13,9},{2,14},{6,2},{... | collective-permute-start | bytes 1179656 | tf_op jit(solution)/shard_map/ppermute | solution.py:308
  14.4 39.4 %collective-permute-start = (bf16[3,512,128]{2,1,0:T(8,128)(2,1)}, bf16[3,512,128]{2,1,0:T(8,128)(2,1)S(1)}, u32[]{:S(2)}, u32[]{:S(2)}) collective-permute-start(bf16[3,512,128]{2,1,0:T(8,128)(2,1)} %get-tuple-element.37), channel_id=1, source_target_pairs={{0,4},{4,8},{1,5},{5,9},{2,6},{6,10},{3,7},{7,11},{16,20},{20,24},... | collective-permute-start | bytes 1179656 | tf_op jit(solution)/shard_map/ppermute | solution.py:308
  17.7 6.6 %copy-start.23 = (s32[1,8]{1,0:T(1,128)S(1)}, s32[1,8]{1,0:T(1,128)}, u32[]{:S(2)}) copy-start(s32[1,8]{1,0:T(1,128)} %param.13) | copy-start | bytes 100
  17.7 6.7 %copy-start.7 = (s32[1,8,8]{2,1,0:T(8,128)S(1)}, s32[1,8,8]{2,1,0:T(8,128)}, u32[]{:S(2)}) copy-start(s32[1,8,8]{2,1,0:T(8,128)} %param.12) | copy-start | bytes 772
  24.3 26.6 %copy-start.11 = (s32[4]{0:T(128)}, s32[4]{0:T(128)S(1)}, u32[]{:S(2)}) copy-start(s32[4]{0:T(128)S(1)} %and_convert_fusion.live_ref) | copy-start | bytes 52
  24.5 26.4 %copy-start.10 = (s32[4]{0:T(128)}, s32[4]{0:T(128)S(1)}, u32[]{:S(2)}) copy-start(s32[4]{0:T(128)S(1)} %and_convert_fusion.1.live_ref) | copy-start | bytes 52
  37.0 1.2 copy-start
  38.2 13.3 %copy-start.16 = (bf16[3,512,128]{2,1,0:T(8,128)(2,1)S(1)}, bf16[3,512,128]{2,1,0:T(8,128)(2,1)}, u32[]{:S(2)}) copy-start(bf16[3,512,128]{2,1,0:T(8,128)(2,1)} %get-tuple-element.38) | copy-start | bytes 1179652
  38.2 15.6 %copy-start.13 = (bf16[3,512,128]{2,1,0:T(8,128)(2,1)S(1)}, bf16[3,512,128]{2,1,0:T(8,128)(2,1)}, u32[]{:S(2)}) copy-start(bf16[3,512,128]{2,1,0:T(8,128)(2,1)} %get-tuple-element.39) | copy-start | bytes 1179652
  45.4 9.2 %collective-permute-start.13 = (bf16[512,128]{1,0:T(8,128)(2,1)}, bf16[512,128]{1,0:T(8,128)(2,1)S(1)}, u32[]{:S(2)}, u32[]{:S(2)}) collective-permute-start(bf16[512,128]{1,0:T(8,128)(2,1)} %get-tuple-element.53), channel_id=1, source_target_pairs={{0,4},{4,8},{8,12},{12,0},{1,5},{5,9},{9,13},{13,1},{2,6},{6,10},{... | collective-permute-start | bytes 393224 | tf_op jit(solution)/shard_map/ppermute | solution.py:308
  47.0 29.4 %copy-start.14 = (bf16[3,512,128]{2,1,0:T(8,128)(2,1)}, bf16[3,512,128]{2,1,0:T(8,128)(2,1)S(1)}, u32[]{:S(2)}) copy-start(bf16[3,512,128]{2,1,0:T(8,128)(2,1)S(1)} %collective-permute-done.10.refs_1_) | copy-start | bytes 1179652
  47.0 24.3 %collective-permute-start.14 = (bf16[512,128]{1,0:T(8,128)(2,1)}, bf16[512,128]{1,0:T(8,128)(2,1)S(1)}, u32[]{:S(2)}, u32[]{:S(2)}) collective-permute-start(bf16[512,128]{1,0:T(8,128)(2,1)} %get-tuple-element.54), channel_id=1, source_target_pairs={{0,8},{4,12},{8,0},{12,4},{1,9},{5,13},{9,1},{13,5},{2,10},{6,14},... | collective-permute-start | bytes 393224 | tf_op jit(solution)/shard_map/ppermute | solution.py:308
  49.5 26.9 %copy-start.15 = (bf16[3,512,128]{2,1,0:T(8,128)(2,1)}, bf16[3,512,128]{2,1,0:T(8,128)(2,1)S(1)}, u32[]{:S(2)}) copy-start(bf16[3,512,128]{2,1,0:T(8,128)(2,1)S(1)} %collective-permute-done.11.refs_2_) | copy-start | bytes 1179652
  49.5 25.5 %collective-permute-start.15 = (bf16[512,128]{1,0:T(8,128)(2,1)}, bf16[512,128]{1,0:T(8,128)(2,1)S(1)}, u32[]{:S(2)}, u32[]{:S(2)}) collective-permute-start(bf16[512,128]{1,0:T(8,128)(2,1)} %get-tuple-element.55), channel_id=1, source_target_pairs={{0,12},{4,0},{8,4},{12,8},{1,13},{5,1},{9,5},{13,9},{2,14},{6,2},{... | collective-permute-start | bytes 393224 | tf_op jit(solution)/shard_map/ppermute | solution.py:308
  51.5 61.4 %collective-permute-start.1 = (bf16[3,512,128]{2,1,0:T(8,128)(2,1)S(1)}, bf16[3,512,128]{2,1,0:T(8,128)(2,1)S(1)}, u32[]{:S(2)}, u32[]{:S(2)}) collective-permute-start(bf16[3,512,128]{2,1,0:T(8,128)(2,1)S(1)} %copy-done.16), channel_id=1, source_target_pairs={{0,8},{12,4},{1,9},{13,5},{2,10},{14,6},{3,11},{15,7},{16,24},{28,... | collective-permute-start | bytes 1179656 | tf_op jit(solution)/shard_map/ppermute | solution.py:308
  53.8 59.1 %copy-start.12 = (bf16[3,512,128]{2,1,0:T(8,128)(2,1)}, bf16[3,512,128]{2,1,0:T(8,128)(2,1)S(1)}, u32[]{:S(2)}) copy-start(bf16[3,512,128]{2,1,0:T(8,128)(2,1)S(1)} %collective-permute-done.refs_1_) | copy-start | bytes 1179652
  53.8 63.4 %collective-permute-start.2 = (bf16[3,512,128]{2,1,0:T(8,128)(2,1)S(1)}, bf16[3,512,128]{2,1,0:T(8,128)(2,1)S(1)}, u32[]{:S(2)}, u32[]{:S(2)}) collective-permute-start(bf16[3,512,128]{2,1,0:T(8,128)(2,1)S(1)} %copy-done.13), channel_id=1, source_target_pairs={{8,4},{12,8},{9,5},{13,9},{10,6},{14,10},{11,7},{15,11},{24,20},{2... | collective-permute-start | bytes 1179656 | tf_op jit(solution)/shard_map/ppermute | solution.py:308
  54.5 21.9 %copy-start.20 = (bf16[512,128]{1,0:T(8,128)(2,1)}, bf16[512,128]{1,0:T(8,128)(2,1)S(1)}, u32[]{:S(2)}) copy-start(bf16[512,128]{1,0:T(8,128)(2,1)S(1)} %collective-permute-done.13.refs_5_) | copy-start | bytes 393220
  54.5 62.7 %collective-permute-start.4 = (bf16[512,128]{1,0:T(8,128)(2,1)}, bf16[512,128]{1,0:T(8,128)(2,1)S(1)}, u32[]{:S(2)}, u32[]{:S(2)}) collective-permute-start(bf16[512,128]{1,0:T(8,128)(2,1)} %get-tuple-element.41), channel_id=1, source_target_pairs={{0,4},{4,8},{1,5},{5,9},{2,6},{6,10},{3,7},{7,11},{16,20},{20,24},... | collective-permute-start | bytes 393224 | tf_op jit(solution)/shard_map/ppermute | solution.py:308
  71.3 5.1 %copy-start.21 = (bf16[512,128]{1,0:T(8,128)(2,1)}, bf16[512,128]{1,0:T(8,128)(2,1)S(1)}, u32[]{:S(2)}) copy-start(bf16[512,128]{1,0:T(8,128)(2,1)S(1)} %collective-permute-done.14.refs_6_) | copy-start | bytes 393220
  71.3 47.2 %collective-permute-start.5 = (bf16[512,128]{1,0:T(8,128)(2,1)}, bf16[512,128]{1,0:T(8,128)(2,1)}, u32[]{:S(2)}, u32[]{:S(2)}) collective-permute-start(bf16[512,128]{1,0:T(8,128)(2,1)} %get-tuple-element.42), channel_id=1, source_target_pairs={{0,8},{12,4},{1,9},{13,5},{2,10},{14,6},{3,11},{15,7},{16,24},{28,... | collective-permute-start | bytes 393224 | tf_op jit(solution)/shard_map/ppermute | solution.py:308
  75.1 1.3 copy-start.22
  75.1 43.4 %collective-permute-start.6 = (bf16[512,128]{1,0:T(8,128)(2,1)}, bf16[512,128]{1,0:T(8,128)(2,1)}, u32[]{:S(2)}, u32[]{:S(2)}) collective-permute-start(bf16[512,128]{1,0:T(8,128)(2,1)} %get-tuple-element.43), channel_id=1, source_target_pairs={{8,4},{12,8},{9,5},{13,9},{10,6},{14,10},{11,7},{15,11},{24,20},{2... | collective-permute-start | bytes 393224 | tf_op jit(solution)/shard_map/ppermute | solution.py:308
  112.9 5.6 %copy-start.17 = (bf16[3,512,128]{2,1,0:T(8,128)(2,1)}, bf16[3,512,128]{2,1,0:T(8,128)(2,1)S(1)}, u32[]{:S(2)}) copy-start(bf16[3,512,128]{2,1,0:T(8,128)(2,1)S(1)} %collective-permute-done.1.refs_2_) | copy-start | bytes 1179652
  112.9 14.0 %collective-permute-start.16 = (bf16[1552,128]{1,0:T(8,128)(2,1)}, bf16[1552,128]{1,0:T(8,128)(2,1)S(1)}, u32[]{:S(2)}, u32[]{:S(2)}) collective-permute-start(bf16[1552,128]{1,0:T(8,128)(2,1)} %get-tuple-element.57), channel_id=1, source_target_pairs={{0,12},{4,0},{8,4},{12,8},{1,13},{5,1},{9,5},{13,9},{2,14},{6,2},{... | collective-permute-start | bytes 1191944 | tf_op jit(solution)/shard_map/ppermute | solution.py:312
  117.2 1.3 copy-start.18
  117.2 21.2 %collective-permute-start.17 = (bf16[1552,128]{1,0:T(8,128)(2,1)}, bf16[1552,128]{1,0:T(8,128)(2,1)S(1)}, u32[]{:S(2)}, u32[]{:S(2)}) collective-permute-start(bf16[1552,128]{1,0:T(8,128)(2,1)} %get-tuple-element.58), channel_id=1, source_target_pairs={{0,8},{4,12},{8,0},{12,4},{1,9},{5,13},{9,1},{13,5},{2,10},{6,14},... | collective-permute-start | bytes 1191944 | tf_op jit(solution)/shard_map/ppermute | solution.py:312
  117.2 0.7 copy-start.19
  117.9 20.5 %collective-permute-start.18 = (bf16[1552,128]{1,0:T(8,128)(2,1)}, bf16[1552,128]{1,0:T(8,128)(2,1)S(1)}, u32[]{:S(2)}, u32[]{:S(2)}) collective-permute-start(bf16[1552,128]{1,0:T(8,128)(2,1)} %get-tuple-element.59), channel_id=1, source_target_pairs={{0,4},{4,8},{8,12},{12,0},{1,5},{5,9},{9,13},{13,1},{2,6},{6,10},{... | collective-permute-start | bytes 1191944 | tf_op jit(solution)/shard_map/ppermute | solution.py:312
  124.3 41.5 %collective-permute-start.7 = (bf16[1552,128]{1,0:T(8,128)(2,1)}, bf16[1552,128]{1,0:T(8,128)(2,1)S(1)}, u32[]{:S(2)}, u32[]{:S(2)}) collective-permute-start(bf16[1552,128]{1,0:T(8,128)(2,1)} %get-tuple-element.45), channel_id=1, source_target_pairs={{4,0},{8,4},{5,1},{9,5},{6,2},{10,6},{7,3},{11,7},{20,16},{24,20},... | collective-permute-start | bytes 1191944 | tf_op jit(solution)/shard_map/ppermute | solution.py:312
  125.6 45.9 %collective-permute-start.8 = (bf16[1552,128]{1,0:T(8,128)(2,1)}, bf16[1552,128]{1,0:T(8,128)(2,1)S(1)}, u32[]{:S(2)}, u32[]{:S(2)}) collective-permute-start(bf16[1552,128]{1,0:T(8,128)(2,1)} %get-tuple-element.46), channel_id=1, source_target_pairs={{4,12},{8,0},{5,13},{9,1},{6,14},{10,2},{7,15},{11,3},{20,28},{24,... | collective-permute-start | bytes 1191944 | tf_op jit(solution)/shard_map/ppermute | solution.py:312
  126.9 11.5 %copy-start.4 = (bf16[1552,128]{1,0:T(8,128)(2,1)}, bf16[1552,128]{1,0:T(8,128)(2,1)S(1)}, u32[]{:S(2)}) copy-start(bf16[1552,128]{1,0:T(8,128)(2,1)S(1)} %collective-permute-done.16.refs_1_) | copy-start | bytes 1191940
  126.9 44.6 %collective-permute-start.9 = (bf16[1552,128]{1,0:T(8,128)(2,1)}, bf16[1552,128]{1,0:T(8,128)(2,1)S(1)}, u32[]{:S(2)}, u32[]{:S(2)}) collective-permute-start(bf16[1552,128]{1,0:T(8,128)(2,1)} %get-tuple-element.47), channel_id=1, source_target_pairs={{4,8},{8,12},{5,9},{9,13},{6,10},{10,14},{7,11},{11,15},{20,24},{2... | collective-permute-start | bytes 1191944 | tf_op jit(solution)/shard_map/ppermute | solution.py:312
  138.4 0.7 copy-start.5
  138.4 0.9 copy-start.6
  165.8 5.7 %copy-start.1 = (bf16[1552,128]{1,0:T(8,128)(2,1)}, bf16[1552,128]{1,0:T(8,128)(2,1)S(1)}, u32[]{:S(2)}) copy-start(bf16[1552,128]{1,0:T(8,128)(2,1)S(1)} %collective-permute-done.7.refs_1_) | copy-start | bytes 1191940
  171.5 0.8 copy-start.2
  171.6 0.9 copy-start.3

commit v2 on v1

--- a/solution.py
+++ b/solution.py
@@ -16,6 +16,7 @@
 ANY = pl.BlockSpec(memory_space=pl.ANY)
 NT = (((1,), (1,)), ((), ()))
 NN = (((1,), (0,)), ((), ()))
+TN = (((0,), (0,)), ((), ()))
 
 
 def mm(lhs, rhs, dims):
@@ -45,53 +46,62 @@
     )(heads, query, key, value)
 
 
-def project_kernel(has_acc, slots, heads_ref, src_ref, *refs):
-    refs = list(refs)
-    grad_ref, w_even, w_odd = refs[:3]
-    weights = jnp.concatenate([w_even[...], w_odd[...]], axis=0)
-    total = mm(grad_ref[...], weights, NT)
-    if has_acc:
-        total = total + refs[3][0]
-        outs = refs[4:]
-        for slot in range(slots):
-            @pl.when(pl.program_id(0) == slot // 2)
-            def _():
-                half = slot % 2
-                outs[slot][...] = total[:, half * HD : (half + 1) * HD].astype(jnp.bfloat16)
-    else:
-        refs[3][0] = total
+def project_kernel(last, heads_ref, src_ref, grad_ref, w_ref, *refs):
+    total = mm(grad_ref[...], w_ref[...], NT)
+    if not refs[1:]:
+        refs[0][0] = total
+        return
+    total = total + refs[0][0]
+    if not last:
+        refs[1][0] = total
+        return
+    outs, held = refs[1:-1], refs[-1]
+    step = pl.program_id(0)
+    for half in range(2):
+        held[2 * step + half] = total[:, half * HD : (half + 1) * HD].astype(jnp.bfloat16)
+
+    @pl.when(step == pl.num_programs(0) - 1)
+    def _():
+        for slot, out in enumerate(outs):
+            out[...] = held[heads_ref[slot]]
 
 
 def project(heads, src, grads, w_out, acc, last):
     rows, feats = grads.shape
     slots = heads.shape[0]
-    steps = slots // 2
+    width = w_out.shape[0]
+    steps = width // (2 * HD)
     in_specs = [
         pl.BlockSpec((rows, feats), lambda s, heads, src: (0, 0)),
-        pl.BlockSpec((HD, feats), lambda s, heads, src: (heads[2 * s], src[0])),
-        pl.BlockSpec((HD, feats), lambda s, heads, src: (heads[2 * s + 1], src[0])),
+        pl.BlockSpec((2 * HD, feats), lambda s, heads, src: (s, src[0])),
     ]
-    args = [grads, w_out, w_out]
+    args = [grads, w_out]
     acc_spec = pl.BlockSpec((1, rows, 2 * HD), lambda s, heads, src: (s, 0, 0))
     if acc is not None:
         in_specs.append(acc_spec)
         args.append(acc)
+    scratch = []
     if last:
         out_shape = [jax.ShapeDtypeStruct((rows, HD), jnp.bfloat16)] * slots
         out_specs = [pl.BlockSpec((rows, HD), lambda s, heads, src: (0, 0))] * slots
+        scratch = [pltpu.VMEM((width // HD, rows, HD), jnp.bfloat16)]
     else:
         out_shape = jax.ShapeDtypeStruct((steps, rows, 2 * HD), jnp.float32)
         out_specs = acc_spec
     return pl.pallas_call(
-        functools.partial(project_kernel, last, slots),
+        functools.partial(project_kernel, last),
         out_shape=out_shape,
         grid_spec=pltpu.PrefetchScalarGridSpec(
-            num_scalar_prefetch=2, grid=(steps,), in_specs=in_specs, out_specs=out_specs
+            num_scalar_prefetch=2,
+            grid=(steps,),
+            in_specs=in_specs,
+            out_specs=out_specs,
+            scratch_shapes=scratch,
         ),
         cost_estimate=pl.CostEstimate(
-            flops=2 * rows * feats * slots * HD,
+            flops=2 * rows * feats * width,
             transcendentals=0,
-            bytes_accessed=2 * (grads.size + slots * HD * feats) + 6 * slots * rows * HD,
+            bytes_accessed=2 * (grads.size + width * feats) + 6 * rows * width,
         ),
         name="project_last" if last else "project_own",
     )(heads, src, *args)
@@ -99,55 +109,52 @@
 
 def attend_kernel(parts, tiles_dev, me_ref, mask_ref, *refs):
     tiles = parts * tiles_dev
+    rows = tiles_dev * TILE
     qkv_refs = refs[:parts]
     grad_refs = refs[parts : 2 * parts]
     outs = refs[2 * parts : 3 * parts]
-    q_s, k_s, v_s, g_s, kt_s, dk_s, dv_s, dq_s, e_s, dp_s, dqt_s, m_s, l_s, d_s = refs[3 * parts :]
+    q_s, k_s, v_s, g_s, dk_s, dv_s, dq_s, e_s, dp_s, ds_s, m_s, l_s, d_s, sems = refs[
+        3 * parts :
+    ]
     score_scale = HD ** (-0.5)
     expo = score_scale * math.log2(math.e)
     me = me_ref[0]
+    copies = []
     for part in range(parts):
-        for sub in range(tiles_dev):
-            tile = part * tiles_dev + sub
-            span = slice(sub * TILE, (sub + 1) * TILE)
-            q_s[tile] = qkv_refs[part][0, span, :]
-            key = qkv_refs[part][1, span, :]
-            k_s[tile] = key
-            kt_s[tile] = key.T
-            v_s[tile] = qkv_refs[part][2, span, :]
-            g_s[tile] = grad_refs[part][span, :]
+        span = pl.ds(part * rows, rows)
+        sources = [qkv_refs[part].at[0], qkv_refs[part].at[1], qkv_refs[part].at[2]]
+        sources.append(grad_refs[part])
+        for j, (source, held) in enumerate(zip(sources, (q_s, k_s, v_s, g_s))):
+            copies.append(pltpu.make_async_copy(source, held.at[span], sems.at[part, j]))
+    for copy in copies:
+        copy.start()
+    for copy in copies:
+        copy.wait()
     dk_s[...] = jnp.zeros_like(dk_s)
     dv_s[...] = jnp.zeros_like(dv_s)
 
-    def place(tile):
-        part = lax.div(tile, tiles_dev)
-        return lax.rem(me - part + parts, parts) * tiles_dev + lax.rem(tile, tiles_dev)
-
-    key_place = [
-        lax.rem(me - tile // tiles_dev + parts, parts) * tiles_dev + tile % tiles_dev
-        for tile in range(tiles)
-    ]
-
-    def query_step(qi, query_sq):
-        own = place(qi)
-        query = q_s[qi]
-        grad = g_s[qi]
-        m_s[...] = jnp.full_like(m_s, -jnp.inf)
-        l_s[...] = jnp.zeros_like(l_s)
-        d_s[...] = jnp.zeros_like(d_s)
-        dqt_s[...] = jnp.zeros_like(dqt_s)
+    def home(part):
+        return lax.rem(me - part + parts, parts) * tiles_dev
+
+    def query_step(part, query_sq):
+        own = home(part)
+        span = pl.ds(pl.multiple_of(part * rows, rows), rows)
+        query = q_s[span, :]
+        grad = g_s[span, :]
         for ki in range(tiles):
-            @pl.when(mask_ref[own, key_place[ki]] != 0)
-            def _(ki=ki):
-                scores = mm(k_s[ki], query, NT)
-                dprob = mm(v_s[ki], grad, NT)
-                top = jnp.max(scores, axis=0, keepdims=True)
-                weight = jnp.exp2((scores - top) * expo)
-                m_s[ki : ki + 1, :] = top
-                l_s[ki : ki + 1, :] = jnp.sum(weight, axis=0, keepdims=True)
-                d_s[ki : ki + 1, :] = jnp.sum(weight * dprob, axis=0, keepdims=True)
-                e_s[ki] = weight
-                dp_s[ki] = dprob
+            place = home(ki // tiles_dev) + ki % tiles_dev
+            scores = mm(k_s[ki * TILE : (ki + 1) * TILE, :], query, NT)
+            dprob = mm(v_s[ki * TILE : (ki + 1) * TILE, :], grad, NT)
+            top = jnp.max(scores, axis=0, keepdims=True)
+            weight = jnp.exp2((scores - top) * expo)
+            for sub in range(tiles_dev):
+                cols = slice(sub * TILE, (sub + 1) * TILE)
+                live = mask_ref[own + sub, place] != 0
+                m_s[ki : ki + 1, cols] = jnp.where(live, top[:, cols], -jnp.inf)
+            l_s[ki : ki + 1, :] = jnp.sum(weight, axis=0, keepdims=True)
+            d_s[ki : ki + 1, :] = jnp.sum(weight * dprob, axis=0, keepdims=True)
+            e_s[ki] = weight
+            dp_s[ki] = dprob
 
         tops = m_s[...]
         factor = jnp.exp2((tops - jnp.max(tops, axis=0, keepdims=True)) * expo)
@@ -155,22 +162,19 @@
         delta = jnp.sum(d_s[...] * factor, axis=0, keepdims=True) / norm
         m_s[...] = factor / norm
         for ki in range(tiles):
-            @pl.when(mask_ref[own, key_place[ki]] != 0)
-            def _(ki=ki):
-                weight = e_s[ki] * m_s[ki : ki + 1, :]
-                dscore = (weight * (dp_s[ki] - delta)).astype(jnp.bfloat16)
-                dv_s[ki] += mm(weight.astype(jnp.bfloat16), grad, NN)
-                dk_s[ki] += mm(dscore, query, NN)
-                dqt_s[...] += mm(kt_s[ki], dscore, NN)
-
-        query_full = dqt_s[...].T * score_scale
-        dq_s[qi] = query_full.astype(jnp.bfloat16)
+            weight = e_s[ki] * m_s[ki : ki + 1, :]
+            dscore = (weight * (dp_s[ki] - delta)).astype(jnp.bfloat16)
+            dv_s[ki] += mm(weight.astype(jnp.bfloat16), grad, NN)
+            dk_s[ki] += mm(dscore, query, NN)
+            ds_s[ki * TILE : (ki + 1) * TILE, :] = dscore
+
+        query_full = mm(ds_s[...], k_s[...], TN) * score_scale
+        dq_s[part] = query_full.astype(jnp.bfloat16)
         return query_sq + jnp.sum(query_full * query_full, axis=0, keepdims=True)
 
-    query_sq = lax.fori_loop(0, tiles, query_step, jnp.zeros((1, HD), jnp.float32))
+    query_sq = lax.fori_loop(0, parts * me_ref[1], query_step, jnp.zeros((1, HD), jnp.float32))
     key_sq = jnp.zeros((1, HD), jnp.float32)
     value_sq = jnp.zeros((1, HD), jnp.float32)
-    rows = tiles_dev * TILE
     for part in range(parts):
         for sub in range(tiles_dev):
             tile = part * tiles_dev + sub
@@ -179,7 +183,7 @@
             key_sq = key_sq + jnp.sum(key_full * key_full, axis=0, keepdims=True)
             value_sq = value_sq + jnp.sum(value_full * value_full, axis=0, keepdims=True)
             low = sub * TILE
-            outs[part][low : low + TILE, :] = dq_s[tile]
+            outs[part][low : low + TILE, :] = dq_s[part, low : low + TILE, :]
             outs[part][rows + low : rows + low + TILE, :] = key_full.astype(jnp.bfloat16)
             outs[part][2 * rows + low : 2 * rows + low + TILE, :] = value_full.astype(jnp.bfloat16)
     row = lax.broadcasted_iota(jnp.int32, (STAT_ROWS, HD), 0)
@@ -211,23 +215,23 @@
     return pl.pallas_call(
         functools.partial(attend_kernel, parts, tiles_dev),
         out_shape=[jax.ShapeDtypeStruct((3 * rows + STAT_ROWS, HD), bf16)] * parts,
-        in_specs=[SMEM, SMEM] + [VMEM] * (2 * parts),
+        in_specs=[SMEM, SMEM] + [ANY] * (2 * parts),
         out_specs=[VMEM] * parts,
         scratch_shapes=[
-            pltpu.VMEM((tiles, TILE, HD), bf16),
-            pltpu.VMEM((tiles, TILE, HD), bf16),
-            pltpu.VMEM((tiles, TILE, HD), bf16),
-            pltpu.VMEM((tiles, TILE, HD), bf16),
-            pltpu.VMEM((tiles, HD, TILE), bf16),
+            pltpu.VMEM((parts * rows, HD), bf16),
+            pltpu.VMEM((parts * rows, HD), bf16),
+            pltpu.VMEM((parts * rows, HD), bf16),
+            pltpu.VMEM((parts * rows, HD), bf16),
             pltpu.VMEM((tiles, TILE, HD), f32),
             pltpu.VMEM((tiles, TILE, HD), f32),
-            pltpu.VMEM((tiles, TILE, HD), bf16),
-            pltpu.VMEM((tiles, TILE, TILE), f32),
-            pltpu.VMEM((tiles, TILE, TILE), f32),
-            pltpu.VMEM((HD, TILE), f32),
-            pltpu.VMEM((tiles, TILE), f32),
-            pltpu.VMEM((tiles, TILE), f32),
-            pltpu.VMEM((tiles, TILE), f32),
+            pltpu.VMEM((parts, rows, HD), bf16),
+            pltpu.VMEM((tiles, TILE, rows), f32),
+            pltpu.VMEM((tiles, TILE, rows), f32),
+            pltpu.VMEM((tiles * TILE, rows), bf16),
+            pltpu.VMEM((tiles, rows), f32),
+            pltpu.VMEM((tiles, rows), f32),
+            pltpu.VMEM((tiles, rows), f32),
+            pltpu.SemaphoreType.DMA((parts, 4)),
         ],
         cost_estimate=pl.CostEstimate(
             flops=pairs * 10 * TILE * TILE * HD,
@@ -337,7 +341,6 @@
         heads.append(base + jnp.clip(dest - first, 0, size - 1).astype(jnp.int32))
         lives.append(((dest >= first) & (dest < first + size)).astype(jnp.int32))
         targets.append(list(range(first, first + size)))
-    me_arr = me.astype(jnp.int32).reshape(1)
     mask = allowed_tiles(key_list[0], key_count[0])
     other = [
         lax.ppermute(output_grad[0], "head", [(s, (s + i) % sides) for s in range(sides)])
@@ -358,7 +361,7 @@
     for k, (head, live, target) in enumerate(zip(heads, lives, targets)):
         slots = acc[k * parts : (k + 1) * parts]
         grads = [slots[0]] + [shift(slots[i], "seq", i, parts, target) for i in range(1, parts)]
-        done = attend(me_arr, mask * live[0], qkv[k], grads)
+        done = attend(jnp.stack([me.astype(jnp.int32), live[0]]), mask, qkv[k], grads)
         back = [done[0]] + [
             shift_back(done[i], "seq", i, parts, target) for i in range(1, parts)
         ]
@@ -518,7 +521,7 @@
 def per_device(*args):
     parts, sides = lax.axis_size("seq"), lax.axis_size("head")
     head_count = args[0].shape[2] // HD
-    if head_count >= parts > 1 and parts % 2 == 0 and sides > 1:
+    if head_count >= parts > 1 and head_count % 2 == 0 and sides > 1:
         return by_heads(*args)
     return by_gather(*args)
 

time: 178 us -> 154 us (0.87)
  Pallas kernels: 68.2 us -> 47.2 us
  waiting for transfers between devices: 52.4 us -> 47.3 us
    pallas_call x2, Pallas kernels: 42.3 us -> 22.9 us  [attend(): pl.pallas_call(functools.partial(attend_kernel, parts, tiles_dev), out_sh...]
    ppermute x6, waiting for transfers between devices: 39.8 us -> 33.9 us  [shift_back(): return lax.ppermute(arr, axis, [(s, (s - step) % size) for s in sources])]
  transfers between devices with their start and end apart: 19 -> 19, of which waited for: 4 -> 5; matrix products, arithmetic and copies ran while one was open for 1% -> 2% of each run, Pallas kernels for 37% -> 29%
where the time goes in v2:
time: 154 us; the launch traced here: 151 us
  starting transfers between devices  47.6 us (31%)
  waiting for transfers between devices  47.3 us (31%)
  Pallas kernels  47.2 us (31%)
  local copies, waits for them, and re-layouts  5.04 us (3%)
  other arithmetic  3.31 us (2%)
    ppermute x12, starting transfers between devices, shift(): return lax.ppermute(arr, axis, pairs)  37.9 us
    ppermute x6, waiting for transfers between devices, shift_back(): return lax.ppermute(arr, axis, [(s, (s - step) % size) for s in sources])  33.9 us
    pallas_call x2, Pallas kernels, attend(): pl.pallas_call(functools.partial(attend_kernel, parts, tiles_dev), out_sh...  22.9 us
    ppermute x1, waiting for transfers between devices, by_heads(): lax.ppermute(output_grad[0], 'head', [(s, (s + i) % sides) for s in range...  13.4 us
    pallas_call x2, Pallas kernels, project(): pl.pallas_call(functools.partial(project_kernel, last), out_shape=out_sha...  12.1 us
    ppermute x6, starting transfers between devices, shift_back(): return lax.ppermute(arr, axis, [(s, (s - step) % size) for s in sources])  8.08 us
    pallas_call x2, Pallas kernels, unpack(): pl.pallas_call(functools.partial(unpack_kernel, parts, rows, count, fresh...  6.13 us
    pallas_call x2, Pallas kernels, pack(): pl.pallas_call(pack_kernel, out_shape=[jax.ShapeDtypeStruct((3, rows, HD)...  6.05 us
  transfers between devices with their start and end apart: 19, of which 5 were waited for; matrix products, arithmetic and copies ran while one was open for 2% of the time, Pallas kernels for 29%

profile of v2, /device:TPU:4, one launch (start us, length us, event | category | flops | bytes accessed | tf_op | source)
XLA Modules:
  0.0 151.3 jit_solution(5574859829193140940)
XLA Ops:
  0.6 1.6 %collective-permute-start.3 = (bf16[512,1536]{1,0:T(8,128)(2,1)}, bf16[512,1536]{1,0:T(8,128)(2,1)S(1)}, u32[]{:S(2)}, u32[]{:S(2)}) collective-permute-start(bf16[512,1536]{1,0:T(8,128)(2,1)} %bitcast.21), channel_id=1, source_target_pairs={{0,2},{2,0},{1,3},{3,1},{4,6},{6,4},{5,7},{7,5},{8,10},{10,8},{9,1... | collective-permute-start | bytes 4718600 | tf_op jit(solution)/shard_map/ppermute | solution.py:346
  2.2 0.6 clamp_add_fusion
  2.8 3.0 %pack_heads.3 = (bf16[3,512,128]{2,1,0:T(8,128)(2,1)}, bf16[3,512,128]{2,1,0:T(8,128)(2,1)}, bf16[3,512,128]{2,1,0:T(8,128)(2,1)}, bf16[3,512,128]{2,1,0:T(8,128)(2,1)}) custom-call(s32[4]{0:T(128)} %get-tuple-element.77.heads_ref, bf16[512,768]{1,0:T(8,128)(2,1)} %bitcast.15, bf16[512,768]{1,0:T(8,128)(2,1)} %bitcast.17, bf16[512,768]{1,0:T(8,128)(2,1)} %bitcast.19), custom_call_target="tpu_custom_call" | custom-call | bytes 3932160 | tf_op jit(solution)/shard_map/pack_heads/pallas_call | solution.py:37
  5.8 1.6 %collective-permute-start.10 = (bf16[3,512,128]{2,1,0:T(8,128)(2,1)}, bf16[3,512,128]{2,1,0:T(8,128)(2,1)S(1)}, u32[]{:S(2)}, u32[]{:S(2)}) collective-permute-start(bf16[3,512,128]{2,1,0:T(8,128)(2,1)} %get-tuple-element.49), channel_id=1, source_target_pairs={{0,4},{4,8},{8,12},{12,0},{1,5},{5,9},{9,13},{13,1},{2,6},{6,10},{... | collective-permute-start | bytes 1179656 | tf_op jit(solution)/shard_map/ppermute | solution.py:312
  7.4 2.6 %collective-permute-start.11 = (bf16[3,512,128]{2,1,0:T(8,128)(2,1)}, bf16[3,512,128]{2,1,0:T(8,128)(2,1)S(1)}, u32[]{:S(2)}, u32[]{:S(2)}) collective-permute-start(bf16[3,512,128]{2,1,0:T(8,128)(2,1)} %get-tuple-element.50), channel_id=1, source_target_pairs={{0,8},{4,12},{8,0},{12,4},{1,9},{5,13},{9,1},{13,5},{2,10},{6,14},... | collective-permute-start | bytes 1179656 | tf_op jit(solution)/shard_map/ppermute | solution.py:312
  10.0 1.3 collective-permute-start.12
  11.3 3.0 %pack_heads.2 = (bf16[3,512,128]{2,1,0:T(8,128)(2,1)}, bf16[3,512,128]{2,1,0:T(8,128)(2,1)}, bf16[3,512,128]{2,1,0:T(8,128)(2,1)}, bf16[3,512,128]{2,1,0:T(8,128)(2,1)}) custom-call(s32[4]{0:T(128)} %get-tuple-element.76.heads_ref, bf16[512,768]{1,0:T(8,128)(2,1)} %bitcast.16, bf16[512,768]{1,0:T(8,128)(2,1)} %bitcast.18, bf16[512,768]{1,0:T(8,128)(2,1)} %bitcast.20), custom_call_target="tpu_custom_call" | custom-call | bytes 3932160 | tf_op jit(solution)/shard_map/pack_heads/pallas_call | solution.py:37
  14.3 2.6 %collective-permute-start = (bf16[3,512,128]{2,1,0:T(8,128)(2,1)}, bf16[3,512,128]{2,1,0:T(8,128)(2,1)S(1)}, u32[]{:S(2)}, u32[]{:S(2)}) collective-permute-start(bf16[3,512,128]{2,1,0:T(8,128)(2,1)} %get-tuple-element.37), channel_id=1, source_target_pairs={{0,4},{4,8},{1,5},{5,9},{2,6},{6,10},{3,7},{7,11},{16,20},{20,24},... | collective-permute-start | bytes 1179656 | tf_op jit(solution)/shard_map/ppermute | solution.py:312
  16.9 0.0 copy-done.8
  17.0 0.6 pad_add_fusion.1.heads_ref
  17.6 5.9 %project_own.1.refs_0_ = f32[3,512,256]{2,1,0:T(8,128)} custom-call(s32[8]{0:T(128)} %pad_add_fusion.1.heads_ref, s32[1]{0:T(128)} %bitcast.8.src_ref, bf16[512,1536]{1,0:T(8,128)(2,1)} %bitcast.22, bf16[768,3072]{1,0:T(8,128)(2,1)} %w_ref.3), custom_call_target="tpu_custom_call" | custom-call | flops 1207959552 | bytes 6291456 | tf_op jit(solution)/shard_map/project_own/pallas_call | solution.py:91
  23.4 0.1 iota_compare_fusion.1
  23.5 0.1 fusion.1
  23.7 13.4 %collective-permute-done.3.grad_ref = bf16[512,1536]{1,0:T(8,128)(2,1)S(1)} collective-permute-done((bf16[512,1536]{1,0:T(8,128)(2,1)}, bf16[512,1536]{1,0:T(8,128)(2,1)S(1)}, u32[]{:S(2)}, u32[]{:S(2)}) %collective-permute-start.3) | collective-permute-done | bytes 1572896 | tf_op jit(solution)/shard_map/ppermute | solution.py:346
  37.0 1.2 copy-done
  38.2 6.2 %project_last.1 = (bf16[512,128]{1,0:T(8,128)(2,1)}, bf16[512,128]{1,0:T(8,128)(2,1)}, bf16[512,128]{1,0:T(8,128)(2,1)}, bf16[512,128]{1,0:T(8,128)(2,1)}, bf16[...) custom-call(s32[8]{0:T(128)} %pad_add_fusion.1.heads_ref, ...), custom_call_target="tpu_custom_call" | custom-call | flops 1207959552 | bytes 6291456 | tf_op jit(solution)/shard_map/project_last/pallas_call | solution.py:91
  44.4 1.6 %collective-permute-start.13 = (bf16[512,128]{1,0:T(8,128)(2,1)}, bf16[512,128]{1,0:T(8,128)(2,1)S(1)}, u32[]{:S(2)}, u32[]{:S(2)}) collective-permute-start(bf16[512,128]{1,0:T(8,128)(2,1)} %get-tuple-element.53), channel_id=1, source_target_pairs={{0,4},{4,8},{8,12},{12,0},{1,5},{5,9},{9,13},{13,1},{2,6},{6,10},{... | collective-permute-start | bytes 393224 | tf_op jit(solution)/shard_map/ppermute | solution.py:312
  46.0 0.0 collective-permute-done.10.refs_1_
  46.0 2.6 %collective-permute-start.14 = (bf16[512,128]{1,0:T(8,128)(2,1)}, bf16[512,128]{1,0:T(8,128)(2,1)S(1)}, u32[]{:S(2)}, u32[]{:S(2)}) collective-permute-start(bf16[512,128]{1,0:T(8,128)(2,1)} %get-tuple-element.54), channel_id=1, source_target_pairs={{0,8},{4,12},{8,0},{12,4},{1,9},{5,13},{9,1},{13,5},{2,10},{6,14},... | collective-permute-start | bytes 393224 | tf_op jit(solution)/shard_map/ppermute | solution.py:312
  48.6 0.0 collective-permute-done.11.refs_2_
  48.6 1.4 collective-permute-start.15
  50.0 0.6 pad_add_fusion.2.me_ref
  50.6 0.6 convert_element_type.10.mask_ref
  51.2 0.7 pad_add_fusion.me_ref
  51.9 0.0 collective-permute-done.12.refs_3_
  51.9 2.3 %collective-permute-start.1 = (bf16[3,512,128]{2,1,0:T(8,128)(2,1)S(1)}, bf16[3,512,128]{2,1,0:T(8,128)(2,1)S(1)}, u32[]{:S(2)}, u32[]{:S(2)}) collective-permute-start(bf16[3,512,128]{2,1,0:T(8,128)(2,1)S(1)} %copy-done.16), channel_id=1, source_target_pairs={{0,8},{12,4},{1,9},{13,5},{2,10},{14,6},{3,11},{15,7},{16,24},{28,... | collective-permute-start | bytes 1179656 | tf_op jit(solution)/shard_map/ppermute | solution.py:312
  54.2 0.0 collective-permute-done.refs_1_
  54.2 0.0 copy-start.12
  54.2 0.0 copy-done.13
  54.2 0.7 collective-permute-start.2
  54.9 0.0 collective-permute-done.13.refs_5_
  54.9 16.3 %collective-permute-start.4 = (bf16[512,128]{1,0:T(8,128)(2,1)}, bf16[512,128]{1,0:T(8,128)(2,1)S(1)}, u32[]{:S(2)}, u32[]{:S(2)}) collective-permute-start(bf16[512,128]{1,0:T(8,128)(2,1)} %get-tuple-element.41), channel_id=1, source_target_pairs={{0,4},{4,8},{1,5},{5,9},{2,6},{6,10},{3,7},{7,11},{16,20},{20,24},... | collective-permute-start | bytes 393224 | tf_op jit(solution)/shard_map/ppermute | solution.py:312
  71.2 0.0 collective-permute-done.14.refs_6_
  71.3 3.7 %collective-permute-start.5 = (bf16[512,128]{1,0:T(8,128)(2,1)}, bf16[512,128]{1,0:T(8,128)(2,1)}, u32[]{:S(2)}, u32[]{:S(2)}) collective-permute-start(bf16[512,128]{1,0:T(8,128)(2,1)} %get-tuple-element.42), channel_id=1, source_target_pairs={{0,8},{12,4},{1,9},{13,5},{2,10},{14,6},{3,11},{15,7},{16,24},{28,... | collective-permute-start | bytes 393224 | tf_op jit(solution)/shard_map/ppermute | solution.py:312
  75.0 0.0 collective-permute-done.15.refs_7_
  75.0 1.3 collective-permute-start.6
  76.3 18.8 %attend_head.3 = (bf16[1552,128]{1,0:T(8,128)(2,1)}, bf16[1552,128]{1,0:T(8,128)(2,1)}, bf16[1552,128]{1,0:T(8,128)(2,1)}, bf16[1552,128]{1,0:T(8,128)(2,1)}) custom-call(s32[2]{0:T(128)} %pad_add_fusion.2.me_ref, s32[8,8]{1,0:T(8,128)} %convert_element_type.10.mask_ref, bf16[3,512,128]{2,1,0:T(8,128)(2,1)} %get-tuple-element.48.refs_0_, ...), custom_call_target="tpu_custom_call" | custom-call | flops 5368709120 | bytes 3670016 | tf_op jit(solution)/shard_map/attend_head/pallas_call | solution.py:215
  95.2 0.0 collective-permute-done.1.refs_2_
  95.2 4.2 %collective-permute-start.16 = (bf16[1552,128]{1,0:T(8,128)(2,1)}, bf16[1552,128]{1,0:T(8,128)(2,1)S(1)}, u32[]{:S(2)}, u32[]{:S(2)}) collective-permute-start(bf16[1552,128]{1,0:T(8,128)(2,1)} %get-tuple-element.57), channel_id=1, source_target_pairs={{0,12},{4,0},{8,4},{12,8},{1,13},{5,1},{9,5},{13,9},{2,14},{6,2},{... | collective-permute-start | bytes 1191944 | tf_op jit(solution)/shard_map/ppermute | solution.py:316
  99.4 0.0 collective-permute-done.2.refs_3_
  99.4 0.0 collective-permute-start.17
  99.4 0.0 collective-permute-done.4.refs_5_
  99.4 0.7 copy-done.19
  100.2 0.6 collective-permute-start.18
  100.8 0.0 collective-permute-done.5.refs_6_
  100.8 0.0 collective-permute-done.6.refs_7_
  100.8 4.1 %attend_head.2 = (bf16[1552,128]{1,0:T(8,128)(2,1)}, bf16[1552,128]{1,0:T(8,128)(2,1)}, bf16[1552,128]{1,0:T(8,128)(2,1)}, bf16[1552,128]{1,0:T(8,128)(2,1)}) custom-call(s32[2]{0:T(128)} %pad_add_fusion.me_ref, s32[8,8]{1,0:T(8,128)} %convert_element_type.10.mask_ref, bf16[3,512,128]{2,1,0:T(8,128)(2,1)} %get-tuple-element.36.refs_0_, ...), custom_call_target="tpu_custom_call" | custom-call | flops 5368709120 | bytes 3670016 | tf_op jit(solution)/shard_map/attend_head/pallas_call | solution.py:215
  104.9 1.3 collective-permute-start.7
  106.2 1.3 collective-permute-start.8
  107.5 1.8 %collective-permute-done.16.refs_1_ = bf16[1552,128]{1,0:T(8,128)(2,1)S(1)} collective-permute-done((bf16[1552,128]{1,0:T(8,128)(2,1)}, bf16[1552,128]{1,0:T(8,128)(2,1)S(1)}, u32[]{:S(2)}, u32[]{:S(2)}) %collective-permute-start.16) | collective-permute-done | bytes 397344 | tf_op jit(solution)/shard_map/ppermute | solution.py:316
  109.3 0.7 collective-permute-start.9
  110.0 23.1 %collective-permute-done.17.refs_2_ = bf16[1552,128]{1,0:T(8,128)(2,1)S(1)} collective-permute-done((bf16[1552,128]{1,0:T(8,128)(2,1)}, bf16[1552,128]{1,0:T(8,128)(2,1)S(1)}, u32[]{:S(2)}, u32[]{:S(2)}) %collective-permute-start.17) | collective-permute-done | bytes 397344 | tf_op jit(solution)/shard_map/ppermute | solution.py:316
  133.1 0.0 collective-permute-done.18.refs_3_
  133.1 0.7 copy-done.5
  133.8 0.2 copy-done.6
  134.0 3.2 %unpack_heads.2 = (bf16[512,768]{1,0:T(8,128)(2,1)}, bf16[512,768]{1,0:T(8,128)(2,1)}, bf16[512,768]{1,0:T(8,128)(2,1)}, f32[6,3]{1,0:T(8,128)}) custom-call(s32[4]{0:T(128)} %get-tuple-element.77.heads_ref, s32[4]{0:T(128)} %copy-done.11, bf16[1552,128]{1,0:T(8,128)(2,1)} %get-tuple-element.56.refs_0_, bf16[1552,128]{1,0:T(8,128)(2,1)} %copy-done.4, ...), custom_call_target="tpu_custom_call" | custom-call | bytes 3145728 | tf_op jit(solution)/shard_map/unpack_heads/pallas_call | solution.py:296
  137.2 2.7 %collective-permute-done.7.refs_1_ = bf16[1552,128]{1,0:T(8,128)(2,1)S(1)} collective-permute-done((bf16[1552,128]{1,0:T(8,128)(2,1)}, bf16[1552,128]{1,0:T(8,128)(2,1)S(1)}, u32[]{:S(2)}, u32[]{:S(2)}) %collective-permute-start.7) | collective-permute-done | bytes 397344 | tf_op jit(solution)/shard_map/ppermute | solution.py:316
  139.9 6.3 %collective-permute-done.8.refs_2_ = bf16[1552,128]{1,0:T(8,128)(2,1)S(1)} collective-permute-done((bf16[1552,128]{1,0:T(8,128)(2,1)}, bf16[1552,128]{1,0:T(8,128)(2,1)S(1)}, u32[]{:S(2)}, u32[]{:S(2)}) %collective-permute-start.8) | collective-permute-done | bytes 397344 | tf_op jit(solution)/shard_map/ppermute | solution.py:316
  146.2 0.0 collective-permute-done.9.refs_3_
  146.2 0.0 copy-done.1
  146.2 0.8 copy-done.2
  147.0 0.1 copy-done.3
  147.1 2.9 %unpack_heads.3 = (bf16[512,768]{1,0:T(8,128)(2,1)}, bf16[512,768]{1,0:T(8,128)(2,1)}, bf16[512,768]{1,0:T(8,128)(2,1)}, f32[6,3]{1,0:T(8,128)}) custom-call(s32[4]{0:T(128)} %get-tuple-element.76.heads_ref, s32[4]{0:T(128)} %copy-done.10, bf16[1552,128]{1,0:T(8,128)(2,1)} %get-tuple-element.44.refs_0_, ...), custom_call_target="tpu_custom_call", output_to_operand_aliasing={{0}: (6, {}), {1}: (7, {}), {2}: (8, {})} | custom-call | bytes 3145728 | tf_op jit(solution)/shard_map/unpack_heads/pallas_call | solution.py:296
  150.0 1.3 copy.17
  (40 shorter events, 0.1 us)
Async XLA Ops:
  0.6 36.4 %collective-permute-start.3 = (bf16[512,1536]{1,0:T(8,128)(2,1)}, bf16[512,1536]{1,0:T(8,128)(2,1)S(1)}, u32[]{:S(2)}, u32[]{:S(2)}) collective-permute-start(bf16[512,1536]{1,0:T(8,128)(2,1)} %bitcast.21), channel_id=1, source_target_pairs={{0,2},{2,0},{1,3},{3,1},{4,6},{6,4},{5,7},{7,5},{8,10},{10,8},{9,1... | collective-permute-start | bytes 4718600 | tf_op jit(solution)/shard_map/ppermute | solution.py:346
  5.8 11.2 %copy-start.8 = (s32[4]{0:T(128)S(1)}, s32[4]{0:T(128)}, u32[]{:S(2)}) copy-start(s32[4]{0:T(128)} %get-tuple-element.76.heads_ref) | copy-start | bytes 52
  5.8 11.2 %copy-start.9 = (s32[4]{0:T(128)S(1)}, s32[4]{0:T(128)}, u32[]{:S(2)}) copy-start(s32[4]{0:T(128)} %get-tuple-element.77.heads_ref) | copy-start | bytes 52
  5.8 40.2 %collective-permute-start.10 = (bf16[3,512,128]{2,1,0:T(8,128)(2,1)}, bf16[3,512,128]{2,1,0:T(8,128)(2,1)S(1)}, u32[]{:S(2)}, u32[]{:S(2)}) collective-permute-start(bf16[3,512,128]{2,1,0:T(8,128)(2,1)} %get-tuple-element.49), channel_id=1, source_target_pairs={{0,4},{4,8},{8,12},{12,0},{1,5},{5,9},{9,13},{13,1},{2,6},{6,10},{... | collective-permute-start | bytes 1179656 | tf_op jit(solution)/shard_map/ppermute | solution.py:312
  7.4 41.2 %collective-permute-start.11 = (bf16[3,512,128]{2,1,0:T(8,128)(2,1)}, bf16[3,512,128]{2,1,0:T(8,128)(2,1)S(1)}, u32[]{:S(2)}, u32[]{:S(2)}) collective-permute-start(bf16[3,512,128]{2,1,0:T(8,128)(2,1)} %get-tuple-element.50), channel_id=1, source_target_pairs={{0,8},{4,12},{8,0},{12,4},{1,9},{5,13},{9,1},{13,5},{2,10},{6,14},... | collective-permute-start | bytes 1179656 | tf_op jit(solution)/shard_map/ppermute | solution.py:312
  10.0 41.9 %collective-permute-start.12 = (bf16[3,512,128]{2,1,0:T(8,128)(2,1)}, bf16[3,512,128]{2,1,0:T(8,128)(2,1)}, u32[]{:S(2)}, u32[]{:S(2)}) collective-permute-start(bf16[3,512,128]{2,1,0:T(8,128)(2,1)} %get-tuple-element.51), channel_id=1, source_target_pairs={{0,12},{4,0},{8,4},{12,8},{1,13},{5,1},{9,5},{13,9},{2,14},{6,2},{... | collective-permute-start | bytes 1179656 | tf_op jit(solution)/shard_map/ppermute | solution.py:312
  14.3 39.8 %collective-permute-start = (bf16[3,512,128]{2,1,0:T(8,128)(2,1)}, bf16[3,512,128]{2,1,0:T(8,128)(2,1)S(1)}, u32[]{:S(2)}, u32[]{:S(2)}) collective-permute-start(bf16[3,512,128]{2,1,0:T(8,128)(2,1)} %get-tuple-element.37), channel_id=1, source_target_pairs={{0,4},{4,8},{1,5},{5,9},{2,6},{6,10},{3,7},{7,11},{16,20},{20,24},... | collective-permute-start | bytes 1179656 | tf_op jit(solution)/shard_map/ppermute | solution.py:312
  17.6 5.9 %copy-start.23 = (s32[1,8]{1,0:T(1,128)S(1)}, s32[1,8]{1,0:T(1,128)}, u32[]{:S(2)}) copy-start(s32[1,8]{1,0:T(1,128)} %param.13) | copy-start | bytes 100
  17.6 6.0 %copy-start.7 = (s32[1,8,8]{2,1,0:T(8,128)S(1)}, s32[1,8,8]{2,1,0:T(8,128)}, u32[]{:S(2)}) copy-start(s32[1,8,8]{2,1,0:T(8,128)} %param.12) | copy-start | bytes 772
  23.5 26.4 %copy-start.11 = (s32[4]{0:T(128)}, s32[4]{0:T(128)S(1)}, u32[]{:S(2)}) copy-start(s32[4]{0:T(128)S(1)} %and_convert_fusion.live_ref) | copy-start | bytes 52
  23.7 27.5 %copy-start.10 = (s32[4]{0:T(128)}, s32[4]{0:T(128)S(1)}, u32[]{:S(2)}) copy-start(s32[4]{0:T(128)S(1)} %and_convert_fusion.1.live_ref) | copy-start | bytes 52
  37.0 1.2 copy-start
  38.2 13.7 %copy-start.16 = (bf16[3,512,128]{2,1,0:T(8,128)(2,1)S(1)}, bf16[3,512,128]{2,1,0:T(8,128)(2,1)}, u32[]{:S(2)}) copy-start(bf16[3,512,128]{2,1,0:T(8,128)(2,1)} %get-tuple-element.38) | copy-start | bytes 1179652
  38.2 16.0 %copy-start.13 = (bf16[3,512,128]{2,1,0:T(8,128)(2,1)S(1)}, bf16[3,512,128]{2,1,0:T(8,128)(2,1)}, u32[]{:S(2)}) copy-start(bf16[3,512,128]{2,1,0:T(8,128)(2,1)} %get-tuple-element.39) | copy-start | bytes 1179652
  44.4 10.5 %collective-permute-start.13 = (bf16[512,128]{1,0:T(8,128)(2,1)}, bf16[512,128]{1,0:T(8,128)(2,1)S(1)}, u32[]{:S(2)}, u32[]{:S(2)}) collective-permute-start(bf16[512,128]{1,0:T(8,128)(2,1)} %get-tuple-element.53), channel_id=1, source_target_pairs={{0,4},{4,8},{8,12},{12,0},{1,5},{5,9},{9,13},{13,1},{2,6},{6,10},{... | collective-permute-start | bytes 393224 | tf_op jit(solution)/shard_map/ppermute | solution.py:312
  46.0 30.3 %copy-start.14 = (bf16[3,512,128]{2,1,0:T(8,128)(2,1)}, bf16[3,512,128]{2,1,0:T(8,128)(2,1)S(1)}, u32[]{:S(2)}) copy-start(bf16[3,512,128]{2,1,0:T(8,128)(2,1)S(1)} %collective-permute-done.10.refs_1_) | copy-start | bytes 1179652
  46.0 25.2 %collective-permute-start.14 = (bf16[512,128]{1,0:T(8,128)(2,1)}, bf16[512,128]{1,0:T(8,128)(2,1)S(1)}, u32[]{:S(2)}, u32[]{:S(2)}) collective-permute-start(bf16[512,128]{1,0:T(8,128)(2,1)} %get-tuple-element.54), channel_id=1, source_target_pairs={{0,8},{4,12},{8,0},{12,4},{1,9},{5,13},{9,1},{13,5},{2,10},{6,14},... | collective-permute-start | bytes 393224 | tf_op jit(solution)/shard_map/ppermute | solution.py:312
  48.6 27.7 %copy-start.15 = (bf16[3,512,128]{2,1,0:T(8,128)(2,1)}, bf16[3,512,128]{2,1,0:T(8,128)(2,1)S(1)}, u32[]{:S(2)}) copy-start(bf16[3,512,128]{2,1,0:T(8,128)(2,1)S(1)} %collective-permute-done.11.refs_2_) | copy-start | bytes 1179652
  48.6 26.4 %collective-permute-start.15 = (bf16[512,128]{1,0:T(8,128)(2,1)}, bf16[512,128]{1,0:T(8,128)(2,1)S(1)}, u32[]{:S(2)}, u32[]{:S(2)}) collective-permute-start(bf16[512,128]{1,0:T(8,128)(2,1)} %get-tuple-element.55), channel_id=1, source_target_pairs={{0,12},{4,0},{8,4},{12,8},{1,13},{5,1},{9,5},{13,9},{2,14},{6,2},{... | collective-permute-start | bytes 393224 | tf_op jit(solution)/shard_map/ppermute | solution.py:312
  51.9 43.3 %collective-permute-start.1 = (bf16[3,512,128]{2,1,0:T(8,128)(2,1)S(1)}, bf16[3,512,128]{2,1,0:T(8,128)(2,1)S(1)}, u32[]{:S(2)}, u32[]{:S(2)}) collective-permute-start(bf16[3,512,128]{2,1,0:T(8,128)(2,1)S(1)} %copy-done.16), channel_id=1, source_target_pairs={{0,8},{12,4},{1,9},{13,5},{2,10},{14,6},{3,11},{15,7},{16,24},{28,... | collective-permute-start | bytes 1179656 | tf_op jit(solution)/shard_map/ppermute | solution.py:312
  54.2 41.0 %copy-start.12 = (bf16[3,512,128]{2,1,0:T(8,128)(2,1)}, bf16[3,512,128]{2,1,0:T(8,128)(2,1)S(1)}, u32[]{:S(2)}) copy-start(bf16[3,512,128]{2,1,0:T(8,128)(2,1)S(1)} %collective-permute-done.refs_1_) | copy-start | bytes 1179652
  54.2 45.2 %collective-permute-start.2 = (bf16[3,512,128]{2,1,0:T(8,128)(2,1)S(1)}, bf16[3,512,128]{2,1,0:T(8,128)(2,1)S(1)}, u32[]{:S(2)}, u32[]{:S(2)}) collective-permute-start(bf16[3,512,128]{2,1,0:T(8,128)(2,1)S(1)} %copy-done.13), channel_id=1, source_target_pairs={{8,4},{12,8},{9,5},{13,9},{10,6},{14,10},{11,7},{15,11},{24,20},{2... | collective-permute-start | bytes 1179656 | tf_op jit(solution)/shard_map/ppermute | solution.py:312
  54.9 21.4 %copy-start.20 = (bf16[512,128]{1,0:T(8,128)(2,1)}, bf16[512,128]{1,0:T(8,128)(2,1)S(1)}, u32[]{:S(2)}) copy-start(bf16[512,128]{1,0:T(8,128)(2,1)S(1)} %collective-permute-done.13.refs_5_) | copy-start | bytes 393220
  54.9 44.5 %collective-permute-start.4 = (bf16[512,128]{1,0:T(8,128)(2,1)}, bf16[512,128]{1,0:T(8,128)(2,1)S(1)}, u32[]{:S(2)}, u32[]{:S(2)}) collective-permute-start(bf16[512,128]{1,0:T(8,128)(2,1)} %get-tuple-element.41), channel_id=1, source_target_pairs={{0,4},{4,8},{1,5},{5,9},{2,6},{6,10},{3,7},{7,11},{16,20},{20,24},... | collective-permute-start | bytes 393224 | tf_op jit(solution)/shard_map/ppermute | solution.py:312
  71.2 5.1 %copy-start.21 = (bf16[512,128]{1,0:T(8,128)(2,1)}, bf16[512,128]{1,0:T(8,128)(2,1)S(1)}, u32[]{:S(2)}) copy-start(bf16[512,128]{1,0:T(8,128)(2,1)S(1)} %collective-permute-done.14.refs_6_) | copy-start | bytes 393220
  71.3 29.5 %collective-permute-start.5 = (bf16[512,128]{1,0:T(8,128)(2,1)}, bf16[512,128]{1,0:T(8,128)(2,1)}, u32[]{:S(2)}, u32[]{:S(2)}) collective-permute-start(bf16[512,128]{1,0:T(8,128)(2,1)} %get-tuple-element.42), channel_id=1, source_target_pairs={{0,8},{12,4},{1,9},{13,5},{2,10},{14,6},{3,11},{15,7},{16,24},{28,... | collective-permute-start | bytes 393224 | tf_op jit(solution)/shard_map/ppermute | solution.py:312
  75.0 1.3 copy-start.22
  75.0 25.7 %collective-permute-start.6 = (bf16[512,128]{1,0:T(8,128)(2,1)}, bf16[512,128]{1,0:T(8,128)(2,1)}, u32[]{:S(2)}, u32[]{:S(2)}) collective-permute-start(bf16[512,128]{1,0:T(8,128)(2,1)} %get-tuple-element.43), channel_id=1, source_target_pairs={{8,4},{12,8},{9,5},{13,9},{10,6},{14,10},{11,7},{15,11},{24,20},{2... | collective-permute-start | bytes 393224 | tf_op jit(solution)/shard_map/ppermute | solution.py:312
  95.2 5.6 %copy-start.17 = (bf16[3,512,128]{2,1,0:T(8,128)(2,1)}, bf16[3,512,128]{2,1,0:T(8,128)(2,1)S(1)}, u32[]{:S(2)}) copy-start(bf16[3,512,128]{2,1,0:T(8,128)(2,1)S(1)} %collective-permute-done.1.refs_2_) | copy-start | bytes 1179652
  95.2 14.1 %collective-permute-start.16 = (bf16[1552,128]{1,0:T(8,128)(2,1)}, bf16[1552,128]{1,0:T(8,128)(2,1)S(1)}, u32[]{:S(2)}, u32[]{:S(2)}) collective-permute-start(bf16[1552,128]{1,0:T(8,128)(2,1)} %get-tuple-element.57), channel_id=1, source_target_pairs={{0,12},{4,0},{8,4},{12,8},{1,13},{5,1},{9,5},{13,9},{2,14},{6,2},{... | collective-permute-start | bytes 1191944 | tf_op jit(solution)/shard_map/ppermute | solution.py:316
  99.4 1.3 copy-start.18
  99.4 33.7 %collective-permute-start.17 = (bf16[1552,128]{1,0:T(8,128)(2,1)}, bf16[1552,128]{1,0:T(8,128)(2,1)S(1)}, u32[]{:S(2)}, u32[]{:S(2)}) collective-permute-start(bf16[1552,128]{1,0:T(8,128)(2,1)} %get-tuple-element.58), channel_id=1, source_target_pairs={{0,8},{4,12},{8,0},{12,4},{1,9},{5,13},{9,1},{13,5},{2,10},{6,14},... | collective-permute-start | bytes 1191944 | tf_op jit(solution)/shard_map/ppermute | solution.py:316
  99.4 0.7 copy-start.19
  100.2 32.9 %collective-permute-start.18 = (bf16[1552,128]{1,0:T(8,128)(2,1)}, bf16[1552,128]{1,0:T(8,128)(2,1)S(1)}, u32[]{:S(2)}, u32[]{:S(2)}) collective-permute-start(bf16[1552,128]{1,0:T(8,128)(2,1)} %get-tuple-element.59), channel_id=1, source_target_pairs={{0,4},{4,8},{8,12},{12,0},{1,5},{5,9},{9,13},{13,1},{2,6},{6,10},{... | collective-permute-start | bytes 1191944 | tf_op jit(solution)/shard_map/ppermute | solution.py:316
  104.9 35.0 %collective-permute-start.7 = (bf16[1552,128]{1,0:T(8,128)(2,1)}, bf16[1552,128]{1,0:T(8,128)(2,1)S(1)}, u32[]{:S(2)}, u32[]{:S(2)}) collective-permute-start(bf16[1552,128]{1,0:T(8,128)(2,1)} %get-tuple-element.45), channel_id=1, source_target_pairs={{4,0},{8,4},{5,1},{9,5},{6,2},{10,6},{7,3},{11,7},{20,16},{24,20},... | collective-permute-start | bytes 1191944 | tf_op jit(solution)/shard_map/ppermute | solution.py:316
  106.2 40.0 %collective-permute-start.8 = (bf16[1552,128]{1,0:T(8,128)(2,1)}, bf16[1552,128]{1,0:T(8,128)(2,1)S(1)}, u32[]{:S(2)}, u32[]{:S(2)}) collective-permute-start(bf16[1552,128]{1,0:T(8,128)(2,1)} %get-tuple-element.46), channel_id=1, source_target_pairs={{4,12},{8,0},{5,13},{9,1},{6,14},{10,2},{7,15},{11,3},{20,28},{24,... | collective-permute-start | bytes 1191944 | tf_op jit(solution)/shard_map/ppermute | solution.py:316
  109.3 23.8 %copy-start.4 = (bf16[1552,128]{1,0:T(8,128)(2,1)}, bf16[1552,128]{1,0:T(8,128)(2,1)S(1)}, u32[]{:S(2)}) copy-start(bf16[1552,128]{1,0:T(8,128)(2,1)S(1)} %collective-permute-done.16.refs_1_) | copy-start | bytes 1191940
  109.3 36.8 %collective-permute-start.9 = (bf16[1552,128]{1,0:T(8,128)(2,1)}, bf16[1552,128]{1,0:T(8,128)(2,1)S(1)}, u32[]{:S(2)}, u32[]{:S(2)}) collective-permute-start(bf16[1552,128]{1,0:T(8,128)(2,1)} %get-tuple-element.47), channel_id=1, source_target_pairs={{4,8},{8,12},{5,9},{9,13},{6,10},{10,14},{7,11},{11,15},{20,24},{2... | collective-permute-start | bytes 1191944 | tf_op jit(solution)/shard_map/ppermute | solution.py:316
  133.1 0.7 copy-start.5
  133.1 0.9 copy-start.6
  139.9 6.3 %copy-start.1 = (bf16[1552,128]{1,0:T(8,128)(2,1)}, bf16[1552,128]{1,0:T(8,128)(2,1)S(1)}, u32[]{:S(2)}) copy-start(bf16[1552,128]{1,0:T(8,128)(2,1)S(1)} %collective-permute-done.7.refs_1_) | copy-start | bytes 1191940
  146.2 0.8 copy-start.2
  146.2 0.9 copy-start.3
